TPU v7x, 32 devices: a whole 2x2x4 slice. The times are simulated.
32 devices in a mesh: clip: 8 (over z, x), freq: 4 (over y, core).
Axes of the slice: x: 2, y: 2, z: 4, core: 2. Of those that a mesh axis runs over, the one named last changes fastest.
Arguments:
- tokens: bfloat16 [24, 1192, 768], P('clip', 'freq'), may hold values from -6 to 6
- kept_counts: int32 [24, 4], P('clip', 'freq'), may hold values from 37 to 298, as said below
- attn_gain: bfloat16 [768], replicated, may hold values from 0.099609375 to 1.8984375
- attn_shift: bfloat16 [768], replicated, may hold values from -3 to 3
- qkv_weight: bfloat16 [768, 2304], replicated, may hold values from -0.3125 to 0.3125
- query_bias: bfloat16 [768], replicated, may hold values from -3 to 3
- value_bias: bfloat16 [768], replicated, may hold values from -3 to 3
- proj_weight: bfloat16 [768, 768], replicated, may hold values from -1.75 to 1.75
- proj_bias: bfloat16 [768], replicated, may hold values from -3 to 3
- mlp_gain: bfloat16 [768], replicated, may hold values from 0.099609375 to 1.8984375
- mlp_shift: bfloat16 [768], replicated, may hold values from -3 to 3
- fc1_weight: bfloat16 [768, 3072], replicated, may hold values from -0.21875 to 0.21875
- fc1_bias: bfloat16 [3072], replicated, may hold values from -3 to 3
- fc2_weight: bfloat16 [3072, 768], replicated, may hold values from -0.15625 to 0.15625
- fc2_bias: bfloat16 [768], replicated, may hold values from -3 to 3
- cotangent: bfloat16 [24, 1192, 768], P('clip', 'freq'), may hold values from -6 to 6
Outputs:
- layer_out: bfloat16 [24, 1192, 768], P('clip', 'freq')
- grad_tokens: float32 [24, 1192, 768], P('clip', 'freq')
- grad_attn_gain: float32 [768], replicated
- grad_attn_shift: float32 [768], replicated
- grad_qkv_weight: float32 [768, 2304], P('clip')
- grad_query_bias: float32 [768], replicated
- grad_value_bias: float32 [768], replicated
- grad_proj_weight: float32 [768, 768], P('clip')
- grad_proj_bias: float32 [768], replicated
- grad_mlp_gain: float32 [768], replicated
- grad_mlp_shift: float32 [768], replicated
- grad_fc1_weight: float32 [768, 3072], P('clip')
- grad_fc1_bias: float32 [3072], replicated
- grad_fc2_weight: float32 [3072, 768], P('clip')
- grad_fc2_bias: float32 [768], replicated
Inputs may be any that keep to these rules, and one draw needn't show every extreme that they name: `kept_counts`: each clip keeps all 298 slots in every group, or between 37 and 149 in each group; clip 0 keeps all; kept tokens fill the first slots of a group.
All inputs are finite; a program needn't handle non-finite values.
Results may differ from a plain program's by a relative error of at most 0.015.
The roundings to bfloat16 on the way count: a program that leaves them out, or rounds other values in their place, can miss the bound.
Values may be sent and summed in bfloat16 or wider, within the bound.
A program may use at most 320 MiB of HBM per device.

v0:
```python
import functools
import math

import jax
import jax.numpy as jnp
from jax import lax
from jax.experimental import pallas as pl
from jax.experimental.pallas import tpu as pltpu
from jax.sharding import PartitionSpec as P

HEADS = 12
DH = 64
EPS = 1e-06
MASKED = -1000000000.0
VMEM_BYTES = 60 * 1024 * 1024

f32 = jnp.float32
bf16 = jnp.bfloat16
NN = (((1,), (0,)), ((), ()))
NT = (((1,), (1,)), ((), ()))
TN = (((0,), (0,)), ((), ()))


def dot(left, right, dims=NN):
    return lax.dot_general(left, right, dims, preferred_element_type=f32)


def center_scale(rows):
    center = rows - jnp.mean(rows, axis=-1, keepdims=True)
    inverse = lax.rsqrt(jnp.mean(center * center, axis=-1, keepdims=True) + EPS)
    return center * inverse, inverse


def norm_back(unit, inverse, gain, grad):
    scaled = grad * gain
    return inverse * (
        scaled
        - jnp.mean(scaled, axis=-1, keepdims=True)
        - unit * jnp.mean(scaled * unit, axis=-1, keepdims=True)
    )


def column_sums(rows):
    return jnp.sum(rows, axis=0, keepdims=True)


def own_lanes(shape, head):
    lane = lax.broadcasted_iota(jnp.int32, shape, len(shape) - 1)
    return lane < DH if head == 0 else lane >= DH


def only(rows, head):
    return jnp.where(own_lanes(rows.shape, head), rows, jnp.zeros_like(rows))


def full(shape):
    return pl.BlockSpec(shape, lambda *ids: (0,) * len(shape))


def params(**more):
    return pltpu.CompilerParams(vmem_limit_bytes=VMEM_BYTES, **more)


def freq_places():
    freq = lax.axis_index("freq")
    core, vert = freq % 2, freq // 2
    return core, vert, {"freq": freq + 1 - 2 * core}, {"freq": (freq + 2) % 4}


def lane_slice(start, size):
    return pl.ds(pl.multiple_of(start, 2 * DH), size)


def row_of(ref):
    return ref[...].astype(f32).reshape(1, ref.shape[0])


def forward_kernel(
    counts,
    kept_ref, tok_ref, qkv_ref, qb_ref, vb_ref, gain_ref, shift_ref, proj_ref, pb_ref, gain2_ref, shift2_ref,
    q_ref, k_ref, v_ref, normed_ref, part_ref, lse_ref, mask_ref, weight_ref, mixed_ref, middle_ref, normed2_ref,
    own, held, mix_send, mix_got, vecs, tok_send, tok_recv, part_send, part_recv,
):
    clips, slots, rows, pairs = counts
    clip = pl.program_id(0)
    pair = pl.program_id(1)
    width = tok_ref.shape[-1]
    half = width // 2
    lanes = 2 * DH
    core, vert, core_dev, vert_dev = freq_places()
    mesh_id = pl.DeviceIdType.MESH

    def copy(kind, index):
        at = {"vert": 0, "core": 1, "diag": 2}[kind]
        return pltpu.make_async_remote_copy(
            src_ref=held.at[index, 0] if kind == "diag" else own.at[index],
            dst_ref=held.at[index, at],
            send_sem=tok_send.at[index, at],
            recv_sem=tok_recv.at[index, at],
            device_id=vert_dev if kind == "vert" else core_dev,
            device_id_type=mesh_id,
        )

    def mix_copy(index, which):
        return pltpu.make_async_remote_copy(
            src_ref=mix_send.at[index, which],
            dst_ref=mix_got.at[index, which],
            send_sem=part_send.at[index, which],
            recv_sem=part_recv.at[index, which],
            device_id=vert_dev,
            device_id_type=mesh_id,
        )

    def project(slot, source):
        unit, _ = center_scale(source.astype(f32))
        normed = (unit * vecs[2:3] + vecs[3:4]).astype(bf16)
        at = slice(slot * rows, (slot + 1) * rows)
        if slot < 2:
            normed_ref[0, at] = normed
            query = (dot(normed, weight_ref[:, :half]) + vecs[0:1, lane_slice(vert * half, half)]).astype(bf16)
            q_ref[0, at] = query * jnp.asarray(DH ** -0.5, bf16)
        both = dot(normed, weight_ref[:, half:])
        k_ref[0, at] = both[:, :half].astype(bf16)
        v_ref[0, at] = (both[:, half:] + vecs[1:2, lane_slice(vert * half, half)]).astype(bf16)
        first = (slots // 16) * 16
        kept = source[first:].astype(f32)[slots - first : slots - first + 1, 0:1] + slots // 2
        lane = lax.broadcasted_iota(jnp.int32, (1, rows), 1).astype(f32)
        return (lane < kept).astype(f32)

    def pass_on(index):
        copy("vert", index).wait_recv()
        copy("diag", index).start()
        copy("vert", index).wait_send()

        @pl.when(index + 1 < clips)
        def more():
            copy("vert", index + 1).start()

    @pl.when((clip == 0) & (pair == 0))
    def enter():
        barrier = pltpu.get_barrier_semaphore()
        for device in (vert_dev, core_dev):
            pl.semaphore_signal(barrier, inc=1, device_id=device, device_id_type=mesh_id)
        first = (slots // 16) * 16
        for index in range(clips):
            kept = (kept_ref[index, 0] - slots // 2).astype(f32).astype(bf16)
            own[index, first:] = jnp.broadcast_to(kept, (rows - first, width))
            own[index, :slots] = tok_ref[index]
        pl.semaphore_wait(barrier, 2)
        copy("vert", 0).start()
        for index in range(clips):
            copy("core", index).start()
        for i, ref in enumerate((qb_ref, vb_ref, gain_ref, shift_ref, pb_ref, gain2_ref, shift2_ref)):
            vecs[i : i + 1] = row_of(ref)
        for part in range(3):
            weight_ref[:, part * half : (part + 1) * half] = qkv_ref[:, lane_slice(part * width + vert * half, half)]

    @pl.when(pair == 0)
    def project_all():
        live_own = project(0, own[clip])
        copy("core", clip).wait_recv()
        live_core = project(2, held[clip, 1])

        @pl.when(clip == 0)
        def first_pass():
            pass_on(clip)

        live_vert = project(1, held[clip, 0])
        copy("diag", clip).wait_recv()
        live_diag = project(3, held[clip, 2])
        mask_ref[0] = jnp.concatenate([live_own, live_vert, live_core, live_diag], axis=1)

    @pl.when((pair == 1) & (clip + 1 < clips))
    def next_pass():
        pass_on(clip + 1)

    def finish(index):
        at = lane_slice(vert * half, half)
        mixed_ref[0, :, at] = mix_own_of(index)
        for which in range(pairs):
            mix_copy(index, which).wait_recv()
            at = lane_slice((1 - vert) * half + which * lanes, lanes)
            mixed_ref[0, :, at] = mix_got[index, which]
        middle = own[index].astype(f32) + (dot(mixed_ref[0], proj_ref[...]) + vecs[4:5])
        middle_ref[0] = middle
        unit, _ = center_scale(middle)
        normed2_ref[0] = (unit * vecs[5:6] + vecs[6:7]).astype(bf16)
        copy("core", index).wait_send()
        copy("diag", index).wait_send()
        for which in range(pairs):
            mix_copy(index, which).wait_send()

    def mix_own_of(index):
        return jnp.concatenate([mix_send[index, pairs + which] for which in range(pairs)], axis=1)

    here = lane_slice(pair * lanes, lanes)
    keys = k_ref[0, :, here]
    values = v_ref[0, :, here]
    live = mask_ref[0] > 0.5
    for slot in (1, 0):
        at = slice(slot * rows, (slot + 1) * rows)
        query = q_ref[0, at, here]
        outs, lses = [], []
        for head in range(2):
            scores = jnp.where(live, dot(only(query, head), keys, NT), MASKED)
            top = jnp.max(scores, axis=1, keepdims=True)
            exps = jnp.exp(scores - top)
            total = jnp.sum(exps, axis=1, keepdims=True)
            outs.append(dot(exps.astype(bf16), values) / total)
            lses.append(top + jnp.log(total))
        first = own_lanes(outs[0].shape, 0)
        mixed = jnp.where(first, outs[0], outs[1]).astype(bf16)
        part_ref[0, at, here] = mixed
        lse_ref[0, at, here] = jnp.where(first, lses[0], lses[1])
        if slot == 1:
            mix_send[clip, pair] = mixed
            mix_copy(clip, pair).start()
        else:
            mix_send[clip, pairs + pair] = mixed

    last = pairs - 1
    for index in range(clips):
        when = (clip == index) & (pair == last) if index == clips - 1 else (clip == index + 1) & (pair == 1)

        @pl.when(when)
        def finish_clip(index=index):
            finish(index)


def forward(kept, tokens, rows, qkv_weight, query_bias, value_bias, gain, shift, proj_weight, proj_bias, gain2, shift2):
    clips, slots, width = tokens.shape
    keys = 4 * rows
    half = width // 2
    pairs = HEADS // 4
    lanes = 2 * DH
    one = pl.Buffered(buffer_count=1)
    block = lambda n, m: pl.BlockSpec((1, n, m), lambda c, p: (c, 0, 0))
    late = lambda n, m: pl.BlockSpec(
        (1, n, m),
        lambda c, p: (jnp.where((c == clips - 1) & (p == pairs - 1), c, jnp.maximum(c - 1, 0)), 0, 0),
    )
    whole = lambda a: pl.BlockSpec(a.shape, lambda c, p: (0,) * a.ndim, pipeline_mode=one)
    shape = jax.ShapeDtypeStruct
    flops = 2 * clips * (rows * width * width * 6 + 2 * rows * keys * width)
    vectors = (query_bias, value_bias, gain, shift)
    return pl.pallas_call(
        functools.partial(forward_kernel, (clips, slots, rows, pairs)),
        grid=(clips, pairs),
        in_specs=[pl.BlockSpec(memory_space=pltpu.SMEM), whole(tokens), whole(qkv_weight)]
        + [whole(v) for v in vectors]
        + [whole(proj_weight)]
        + [whole(v) for v in (proj_bias, gain2, shift2)],
        out_specs=[
            block(2 * rows, half), block(keys, half), block(keys, half), block(2 * rows, width),
            block(2 * rows, half), block(2 * rows, half), block(1, keys),
            pl.BlockSpec((width, 3 * half), lambda c, p: (0, 0), pipeline_mode=one),
            late(rows, width), late(rows, width), late(rows, width),
        ],
        out_shape=[
            shape((clips, 2 * rows, half), bf16),
            shape((clips, keys, half), bf16),
            shape((clips, keys, half), bf16),
            shape((clips, 2 * rows, width), bf16),
            shape((clips, 2 * rows, half), bf16),
            shape((clips, 2 * rows, half), f32),
            shape((clips, 1, keys), f32),
            shape((width, 3 * half), bf16),
            shape((clips, rows, width), bf16),
            shape((clips, rows, width), f32),
            shape((clips, rows, width), bf16),
        ],
        scratch_shapes=[
            pltpu.VMEM((clips, rows, width), bf16),
            pltpu.VMEM((clips, 3, rows, width), bf16),
            pltpu.VMEM((clips, 2 * pairs, rows, lanes), bf16),
            pltpu.VMEM((clips, pairs, rows, lanes), bf16),
            pltpu.VMEM((8, width), f32),
            pltpu.SemaphoreType.DMA((clips, 3)),
            pltpu.SemaphoreType.DMA((clips, 3)),
            pltpu.SemaphoreType.DMA((clips, pairs)),
            pltpu.SemaphoreType.DMA((clips, pairs)),
        ],
        compiler_params=params(collective_id=0, has_side_effects=True),
        cost_estimate=pl.CostEstimate(
            flops=flops, bytes_accessed=40_000_000, transcendentals=clips * rows * keys * HEADS
        ),
        name="forward",
    )(kept, tokens, qkv_weight, *vectors, proj_weight, proj_bias, gain2, shift2)


def mlp_kernel(
    counts,
    kept_ref, n2_ref, middle_ref, cot_ref, mixed_ref, fc1_ref, b1_ref, fc2_ref, b2_ref, gain_ref, proj_ref,
    out_ref, dfc1_ref, dfc2_ref, dproj_ref, db1_ref, small_ref, gmid_ref, gmixed_ref,
    n2t_ref, grad_ref, out_acc, dn_acc, hidden_ref, dact_ref, active_ref, dhid_ref, biases,
):
    clips, slots, rows, tile = counts
    step = pl.program_id(0)
    width = n2_ref.shape[-1]
    chunk = fc1_ref.shape[-1]
    total = clips * rows

    def live_rows(clip, size):
        slot = lax.broadcasted_iota(jnp.int32, (size, 1), 0)
        return (slot < kept_ref[clip, 0]).astype(f32)

    @pl.when(step == 0)
    def start():
        n2t_ref[...] = n2_ref[...].T
        first = (slots // 16) * 16
        for clip in range(clips):
            begin = clip * rows
            grad_ref[begin + first : begin + rows] = jnp.zeros((rows - first, width), bf16)
            grad_ref[begin : begin + slots] = cot_ref[clip] * live_rows(clip, slots).astype(bf16)
        all_biases = row_of(b1_ref)
        for i in range(all_biases.shape[1] // chunk):
            biases[i : i + 1] = all_biases[:, i * chunk : (i + 1) * chunk]
        out_acc[...] = jnp.zeros_like(out_acc)
        dn_acc[...] = jnp.zeros_like(dn_acc)

    hidden_ref[...] = dot(n2_ref[...], fc1_ref[...])
    dact_ref[...] = dot(grad_ref[...], fc2_ref[...], NT)
    bias = biases[pl.ds(step, 1), :]

    def gelu_tile(index, sums):
        at = pl.ds(pl.multiple_of(index * tile, tile), tile)
        hidden = hidden_ref[at, :] + bias
        cdf = 0.5 * (1.0 + lax.erf(hidden * (0.5 ** 0.5)))
        active_ref[at, :] = (hidden * cdf).astype(bf16)
        slope = cdf + hidden * (jnp.exp(-0.5 * hidden * hidden) * (1.0 / math.sqrt(2.0 * math.pi)))
        dhid = (dact_ref[at, :] * slope).astype(bf16)
        dhid_ref[at, :] = dhid
        return sums + dhid.astype(f32)

    sums = lax.fori_loop(0, total // tile, gelu_tile, jnp.zeros((tile, chunk), f32))
    db1_ref[...] = column_sums(sums)
    active = active_ref[...]
    dhid = dhid_ref[...]
    out_acc[...] += dot(active, fc2_ref[...])
    dn_acc[...] += dot(dhid, fc1_ref[...], NT)
    dfc1_ref[0] = dot(n2t_ref[...], dhid).astype(bf16)
    dfc2 = dot(active, grad_ref[...], TN).astype(bf16)
    half = width // 2
    dfc2_ref[0] = dfc2[:, :half]
    dfc2_ref[1] = dfc2[:, half:]

    @pl.when(step == pl.num_programs(0) - 1)
    def finish():
        gain = row_of(gain_ref)
        bias2 = row_of(b2_ref)
        sum_gain = jnp.zeros((1, width), f32)
        sum_shift = jnp.zeros((1, width), f32)
        sum_grad = jnp.zeros((1, width), f32)
        sum_proj = jnp.zeros((1, width), f32)
        for clip in range(clips):
            at = slice(clip * rows, (clip + 1) * rows)
            middle = middle_ref[at]
            layer = middle[:slots] + (out_acc[clip * rows : clip * rows + slots] + bias2)
            out_ref[clip] = (live_rows(clip, slots) * layer).astype(bf16)
            unit, inverse = center_scale(middle)
            grad = dn_acc[at]
            out_grad = grad_ref[at].astype(f32)
            gmid = out_grad + norm_back(unit, inverse, gain, grad)
            gmid_ref[at] = gmid
            low = gmid.astype(bf16)
            dhid_ref[at, :width] = low
            gmixed_ref[at] = dot(low, proj_ref[...], NT).astype(bf16)
            sum_gain += column_sums(grad * unit)
            sum_shift += column_sums(grad)
            sum_grad += column_sums(out_grad)
            sum_proj += column_sums(low.astype(f32))
        dproj = dot(mixed_ref[...], dhid_ref[:, :width], TN).astype(bf16)
        dproj_ref[0] = dproj[:, :half]
        dproj_ref[1] = dproj[:, half:]
        small_ref[0:1] = sum_gain
        small_ref[1:2] = sum_shift
        small_ref[2:3] = sum_grad
        small_ref[3:4] = sum_proj


def mlp(kept, n2, middle, cot, mixed, fc1, b1, fc2, b2, gain, proj, rows):
    clips, slots, _ = cot.shape
    total, width = n2.shape
    hidden = fc1.shape[1]
    chunk = 768
    steps = hidden // chunk
    half = steps // 2
    tile = 16
    whole = lambda a: pl.BlockSpec(a.shape, lambda j: (0,) * a.ndim, pipeline_mode=one)
    one = pl.Buffered(buffer_count=1)
    big = pl.BlockSpec((total, width), lambda j: (0, 0), pipeline_mode=one)
    return pl.pallas_call(
        functools.partial(mlp_kernel, (clips, slots, rows, tile)),
        grid=(steps,),
        in_specs=[
            pl.BlockSpec(memory_space=pltpu.SMEM),
            big, big, whole(cot), big,
            pl.BlockSpec((width, chunk), lambda j: (0, j)),
            whole(b1),
            pl.BlockSpec((chunk, width), lambda j: (j, 0)),
            whole(b2), whole(gain), whole(proj),
        ],
        out_specs=[
            full((clips, slots, width)),
            pl.BlockSpec((1, width, chunk), lambda j: (j // half, 0, j % half)),
            pl.BlockSpec((2, chunk, width // 2), lambda j: (0, j, 0)),
            full((2, width, width // 2)),
            pl.BlockSpec((1, chunk), lambda j: (0, j)),
            full((8, width)),
            full((total, width)),
            full((total, width)),
        ],
        out_shape=[
            jax.ShapeDtypeStruct((clips, slots, width), bf16),
            jax.ShapeDtypeStruct((2, width, hidden // 2), bf16),
            jax.ShapeDtypeStruct((2, hidden, width // 2), bf16),
            jax.ShapeDtypeStruct((2, width, width // 2), bf16),
            jax.ShapeDtypeStruct((1, hidden), f32),
            jax.ShapeDtypeStruct((8, width), f32),
            jax.ShapeDtypeStruct((total, width), f32),
            jax.ShapeDtypeStruct((total, width), bf16),
        ],
        scratch_shapes=[
            pltpu.VMEM((width, total), bf16),
            pltpu.VMEM((total, width), bf16),
            pltpu.VMEM((total, width), f32),
            pltpu.VMEM((total, width), f32),
            pltpu.VMEM((total, chunk), f32),
            pltpu.VMEM((total, chunk), f32),
            pltpu.VMEM((total, chunk), bf16),
            pltpu.VMEM((total, chunk), bf16),
            pltpu.VMEM((8, chunk), f32),
        ],
        compiler_params=params(),
        cost_estimate=pl.CostEstimate(
            flops=12 * total * width * hidden, bytes_accessed=40_000_000, transcendentals=2 * total * hidden
        ),
        name="mlp",
    )(kept, n2, middle, cot, mixed, fc1, b1, fc2, b2, gain, proj)


def sum_arrays(width, hidden, clip_size):
    rows = width // clip_size
    tall = hidden // clip_size
    first, second = (0, 1, 2), (1, 0, 2)
    cut = 5 * width // 6
    return [
        ("fc1", 0, rows, hidden // 4, first),
        ("fc2", 0, tall // 2, width // 2, second),
        ("fc1", hidden // 4, rows, hidden // 4, first),
        ("fc2", tall // 2, tall // 2, width // 2, second),
        ("proj", 0, rows, width // 2, PROJ_ORDER),
        ("qkv", 0, rows // 2, cut, QKV_ORDERS[0]),
        ("qkv", cut, rows // 2, 3 * width // 2 - cut, QKV_ORDERS[1]),
    ]


PROJ_ORDER = (1, 0, 2)
QKV_ORDERS = ((1, 0, 2), (0, 1, 2))
SUM_STEPS = {
    3: [("end", 4, 0), ("start", 4, 1)],
    4: [("end", 0, 0), ("start", 0, 1), ("end", 1, 0), ("end", 2, 0), ("end", 3, 0)],
    5: [("start", 1, 1)],
    6: [("end", 4, 1)],
    8: [("start", 2, 1)],
    9: [("end", 0, 1), ("start", 0, 2)],
    10: [("end", 1, 1)],
    11: [("start", 3, 1)],
    12: [("end", 0, 2), ("start", 0, 3), ("start", 1, 2)],
    13: [("end", 2, 1)],
    14: [("start", 4, 2)],
    15: [("end", 1, 2), ("start", 1, 3)],
    16: [("end", 0, 3), ("start", 0, 4), ("start", 2, 2), ("end", 4, 2)],
    17: [("start", 4, 3)],
    18: [("end", 3, 1), ("start", 3, 2)],
    19: [("end", 0, 4), ("start", 0, 5), ("end", 1, 3), ("start", 1, 4), ("end", 4, 3),
        ("start", 4, 4)],
    20: [("end", 0, 5), ("end", 2, 2), ("start", 2, 3)],
    21: [("end", 1, 4), ("start", 1, 5), ("end", 3, 2), ("start", 3, 3), ("end", 4, 4),
        ("start", 4, 5)],
    22: [("end", 1, 5), ("end", 4, 5)],
    23: [("end", 6, 0), ("start", 6, 1), ("end", 5, 0), ("start", 5, 1), ("end", 2, 3),
        ("start", 2, 4), ("end", 3, 3), ("start", 3, 4), ("input", 2, 0), ("end", 6, 1),
        ("start", 6, 2), ("end", 2, 4), ("start", 2, 5), ("vec", 0, 0), ("end", 5, 1),
        ("start", 5, 2), ("end", 2, 5), ("end", 3, 4), ("start", 3, 5), ("end", 6, 2),
        ("start", 6, 3), ("vec", 1, 0), ("end", 3, 5), ("end", 5, 2), ("start", 5, 3), ("vec", 2, 0),
        ("end", 6, 3), ("start", 6, 4), ("end", 5, 3), ("start", 5, 4), ("vec", 3, 0), ("end", 6, 4),
        ("start", 6, 5), ("end", 6, 5), ("end", 5, 4), ("start", 5, 5), ("vec", 4, 0), ("end", 5, 5)],
}


def backward_kernel(
    meta,
    q_ref, k_ref, v_ref, mask_ref, part_ref, lse_ref, normed_ref, weight_ref, tok_ref, gmid_ref, gain_ref,
    small_ref, db1_ref, gmixed_ref, dfc1_ref, dfc2_ref, dproj_ref,
    gtok_ref, fc1_out, fc2_out, proj_out, qkv_out, vec_out,
    *scratch,
):
    clips, slots, rows, bits, pairs, arrays = meta
    width = weight_ref.shape[0]
    half = width // 2
    lanes = 2 * DH
    step = pl.program_id(0)
    places = step_places(clips, pairs)
    mesh_id = pl.DeviceIdType.MESH
    count = len(arrays)

    scratch = list(scratch)
    take = lambda n: [scratch.pop(0) for _ in range(n)]
    (grad_all, packed, kv_acc, kv_send, kv_got, acc, dn_send, dn_got, dw_acc, bias_acc, vec_sum, vec_got) = take(12)
    own_bufs = dict(zip(("fc1", "fc2", "proj"), take(3)))
    dw_low = {5: scratch.pop(0), 6: scratch.pop(0)}
    stage_bufs = [take(bits + 1) for _ in arrays]
    vert_bufs = take(5)
    full_bufs = take(count)
    (grad_sem, grad_out, grad_in, kv_out, kv_in, dn_out, dn_in, sum_out, sum_in, own_sem, vec_out_sem, vec_in_sem) = take(12)

    core, vert, core_dev, vert_dev = freq_places()
    place = lax.axis_index("clip")
    bit_at = [(place // 2 ** b) % 2 for b in range(bits)]
    clip_dev = [{"clip": place + (1 - 2 * bit_at[b]) * 2 ** b} for b in range(bits)]

    def remote(src, dst, send, recv, device):
        return pltpu.make_async_remote_copy(
            src_ref=src, dst_ref=dst, send_sem=send, recv_sem=recv, device_id=device, device_id_type=mesh_id
        )

    def grad_own(clip):
        src = gmixed_ref.at[clip, :, lane_slice(vert * half, half)]
        return pltpu.make_async_copy(src, grad_all.at[0, clip], grad_sem.at[clip])

    def grad_vert(clip):
        src = gmixed_ref.at[clip, :, lane_slice((1 - vert) * half, half)]
        return remote(src, grad_all.at[1, clip], grad_out.at[clip], grad_in.at[clip], vert_dev)

    def kv_copy(clip, pair):
        return remote(
            kv_send.at[pair], kv_got.at[clip, pair], kv_out.at[clip, pair], kv_in.at[clip, pair], core_dev
        )

    def dn_copy(clip):
        return remote(dn_send.at[clip], dn_got.at[clip], dn_out.at[clip], dn_in.at[clip], vert_dev)

    every = (slice(None),) * bits

    def piece(a, who):
        name, at, r, width_a, _ = arrays[a]
        if name == "fc1":
            return dfc1_ref.at[(who,) + every + (slice(None), pl.ds(at, width_a))]
        if name == "fc2":
            return dfc2_ref.at[(who,) + every + (pl.ds(at, r), slice(None))]
        if name == "proj":
            return dproj_ref.at[who]
        return dw_low[a].at[who]

    def chosen(a, stage, index_of):
        order = arrays[a][4]
        left = [b for b in range(bits)[::-1] if b not in order[: stage - 1]]
        bit = order[stage - 1]
        at = (slice(None),) * left.index(bit) + (index_of(bit),)
        return stage_bufs[a][stage - 1].at[at]

    def stage_copy(a, stage):
        sems = (sum_out.at[a, stage], sum_in.at[a, stage])
        full, packed_array = full_bufs[a], arrays[a][0] == "qkv"
        if stage == 0:
            return remote(piece(a, 1 - core), stage_bufs[a][0], *sems, core_dev)
        if stage <= bits:
            src = chosen(a, stage, lambda bit: 1 - bit_at[bit])
            return remote(src, stage_bufs[a][stage], *sems, clip_dev[arrays[a][4][stage - 1]])
        if stage == bits + 1:
            dst = full.at[core, vert] if packed_array else vert_bufs[a]
            return remote(stage_bufs[a][bits], dst, *sems, vert_dev)
        return remote(full.at[core], full.at[core], *sems, core_dev)

    def own_copy(a):
        return pltpu.make_async_copy(piece(a, core), own_bufs[arrays[a][0]], own_sem.at[a])

    def add_blocks(dst, src, lead):
        if lead == 0:
            dst[...] = dst[...] + src[...]
            return

        def add_one(i, carry):
            at = tuple((i // 2 ** (lead - 1 - j)) % 2 for j in range(lead))
            dst[at] = dst[at] + src[at]
            return carry

        lax.fori_loop(0, 2 ** lead, add_one, 0)

    def stage_end(a, stage):
        name = arrays[a][0]
        stage_copy(a, stage).wait_recv()
        if stage == 0:
            if name == "qkv":
                add_blocks(stage_bufs[a][0], dw_low[a].at[core], bits)
            else:
                own_copy(a).wait()
                add_blocks(stage_bufs[a][0], own_bufs[name], bits)
                if a + 2 < 4:
                    own_copy(a + 2).start()
        elif stage <= bits:
            add_blocks(stage_bufs[a][stage], chosen(a, stage, lambda bit: bit_at[bit]), bits - stage)
            if stage == bits and name == "qkv":
                full_bufs[a][core, vert] = stage_bufs[a][bits][...]
        elif stage == bits + 1 and name != "qkv":
            full_bufs[a][core] = stage_bufs[a][bits][...] + vert_bufs[a][...]

    def vec_copy(hop):
        device = core_dev if hop == 0 else vert_dev if hop == 1 else clip_dev[hop - 2]
        return remote(vec_sum.at[hop], vec_got.at[hop], vec_out_sem.at[hop], vec_in_sem.at[hop], device)

    def vec_end(hop):
        vec_copy(hop).wait_recv()
        vec_sum[hop + 1] = vec_sum[hop] + vec_got[hop]
        if hop < bits + 1:
            vec_copy(hop + 1).start()

    def perform(action):
        kind, a, stage = action
        if kind == "vec":
            vec_end(a)
        elif kind == "start":
            stage_copy(a, stage).start()
        else:
            stage_end(a, stage)

    @pl.when(step == 0)
    def enter():
        barrier = pltpu.get_barrier_semaphore()
        for clip in range(clips):
            grad_own(clip).start()
        for device in [core_dev, vert_dev] + clip_dev:
            pl.semaphore_signal(barrier, inc=1, device_id=device, device_id_type=mesh_id)
        pl.semaphore_wait(barrier, 2 + bits)
        for clip in range(clips):
            grad_vert(clip).start()
        for a in range(5):
            stage_copy(a, 0).start()
        for a in (0, 1, 4):
            own_copy(a).start()
        vec_sum[0] = jnp.zeros_like(vec_sum[0])
        vec_sum[0, 4:8] = small_ref[0:4]
        for i in range(db1_ref.shape[1] // width):
            vec_sum[0, 8 + i : 9 + i] = db1_ref[0:1, i * width : (i + 1) * width]

    for at in sorted(SUM_STEPS):
        if at < places["end"]:
            @pl.when(step == at)
            def run(at=at):
                for action in SUM_STEPS[at]:
                    perform(action)

    def attend():
        index = attention_index(step, places)
        clip = index // (2 * pairs)
        slot = (index // pairs) % 2
        pair = index % pairs

        @pl.when((pair == 0) & (slot == 0))
        def own_grads():
            grad_own(clip).wait()

        @pl.when((pair == 0) & (slot == 1))
        def vert_grads():
            grad_vert(clip).wait_recv()

        query = q_ref[0]
        keys = k_ref[0]
        values = v_ref[0]
        grad = grad_all[slot, clip, :, lane_slice(pair * lanes, lanes)]
        live = mask_ref[0] > 0.5
        product = grad.astype(f32) * part_ref[0].astype(f32)
        dqs, dk, dv = [], None, None
        for head in range(2):
            own_query = only(query, head)
            own_grad = only(grad, head)
            scores = jnp.where(live, dot(own_query, keys, NT), MASKED)
            probs = jnp.exp(scores - lse_ref[0, :, head * DH : head * DH + 1])
            delta = jnp.sum(only(product, head), axis=1, keepdims=True)
            dscores = (probs * (dot(own_grad, values, NT) - delta)).astype(bf16)
            dqs.append(dot(dscores, keys))
            more_k = dot(dscores, own_query, TN)
            more_v = dot(probs.astype(bf16), own_grad, TN)
            dk = more_k if dk is None else dk + more_k
            dv = more_v if dv is None else dv + more_v
        first = own_lanes(dqs[0].shape, 0)
        dq = (jnp.where(first, dqs[0], dqs[1]) * DH ** -0.5).astype(bf16)
        at = pl.ds(pl.multiple_of(slot * rows, rows), rows)
        packed[clip, at, lane_slice(pair * lanes, lanes)] = dq

        @pl.when(slot == 0)
        def keep():
            kv_acc[pair, 0] = dk
            kv_acc[pair, 1] = dv

        @pl.when(slot == 1)
        def send():
            @pl.when(clip > 0)
            def free():
                kv_copy(clip - 1, pair).wait_send()

            for part, value in enumerate((dk, dv)):
                low = (kv_acc[pair, part] + value).astype(bf16)
                packed[clip, :, lane_slice((part + 1) * half + pair * lanes, lanes)] = low[: 2 * rows]
                kv_send[pair, part] = low[2 * rows :]
            kv_copy(clip, pair).start()

    is_attention = step < places["projections"][-1]
    for at in places["projections"][:-1]:
        is_attention = is_attention & (step != at)
    pl.when(is_attention)(attend)

    for clip in range(clips):
        @pl.when(step == places["projections"][clip])
        def projections(clip=clip):
            for pair in range(pairs):
                kv_copy(clip, pair).wait_recv()
                for part in range(2):
                    at = slice((part + 1) * half + pair * lanes, (part + 1) * half + (pair + 1) * lanes)
                    packed[clip, :, at] = packed[clip, :, at] + kv_got[clip, pair, part]
            grads = packed[clip]
            back = dot(grads, weight_ref[...], NT)
            acc[clip] = back[:rows]
            dn_send[clip] = back[rows:].astype(bf16)
            dn_copy(clip).start()
            more = dot(normed_ref[0], grads, TN)
            sum_q = column_sums(grads[:, :half].astype(f32))
            sum_v = column_sums(grads[:, 2 * half :].astype(f32))
            if clip == 0:
                dw_acc[...] = more
                bias_acc[0:1] = sum_q
                bias_acc[1:2] = sum_v
            elif clip < clips - 1:
                dw_acc[...] += more
                bias_acc[0:1] += sum_q
                bias_acc[1:2] += sum_v
            else:
                low = (dw_acc[...] + more).astype(bf16)
                for a, buf in dw_low.items():
                    _, at, r, width_a, _ = arrays[a]
                    for block in range(2 ** bits):
                        index = tuple((block >> b) & 1 for b in range(bits)[::-1])
                        for who in range(2):
                            start = (2 * block + who) * r
                            buf[(who,) + index] = low[start : start + r, at : at + width_a]
                    stage_copy(a, 0).start()
                mine = lane_slice(vert * half, half)
                vec_sum[0, 2:3, mine] = bias_acc[0:1] + sum_q
                vec_sum[0, 3:4, mine] = bias_acc[1:2] + sum_v

    def inputs(clip):
        dn_copy(clip).wait_recv()
        grad = acc[clip] + dn_got[clip].astype(f32)
        unit, inverse = center_scale(tok_ref[0].astype(f32))
        result = gmid_ref[0][:slots] + norm_back(unit, inverse, row_of(gain_ref), grad[:slots])
        gtok_ref[0] = result
        vec_sum[0, 0:1] += column_sums(grad[:slots] * unit)
        vec_sum[0, 1:2] += column_sums(grad[:slots])
        if clip == clips - 1:
            vec_copy(0).start()

    for clip in range(clips - 1):
        pl.when(step == places["inputs"] + clip)(functools.partial(inputs, clip))

    @pl.when(step == places["end"])
    def finish():
        for kind, a, stage in SUM_STEPS[places["end"]]:
            if kind == "input":
                inputs(clips - 1)
            else:
                perform((kind, a, stage))
        for a, (name, at, r, width_a, _) in enumerate(arrays):
            for who in range(2):
                full = full_bufs[a]
                if name == "fc1":
                    start = who * fc1_out.shape[1] // 2 + at
                    fc1_out[:, start : start + width_a] = full[who]
                elif name == "fc2":
                    fc2_out[at : at + r, who * width_a : (who + 1) * width_a] = full[who]
                elif name == "proj":
                    proj_out[:, who * width_a : (who + 1) * width_a] = full[who]
                else:
                    for side in range(2):
                        for start in range(0, width_a, lanes):
                            part, inside = divmod(at + start, half)
                            to = part * width + side * half + inside
                            qkv_out[who * r : (who + 1) * r, to : to + lanes] = full[who, side, :, start : start + lanes]
        vec_out[...] = vec_sum[bits + 2]
        for a in range(count):
            for stage in range(bits + 3):
                stage_copy(a, stage).wait_send()
        for clip in range(clips):
            grad_vert(clip).wait_send()
            dn_copy(clip).wait_send()
        for pair in range(pairs):
            kv_copy(clips - 1, pair).wait_send()
        for hop in range(bits + 2):
            vec_copy(hop).wait_send()


def step_places(clips, pairs):
    of_clip = 2 * pairs
    projections = [of_clip * (c + 1) + 2 + c for c in range(clips - 1)] + [of_clip * clips + clips - 1]
    inputs = projections[-1] + 1
    return {"projections": projections, "inputs": inputs, "end": inputs + clips - 1}


def attention_index(step, places):
    index = step
    for at in places["projections"][:-1]:
        index = index - (step > at).astype(jnp.int32)
    return index


def backward(q, k, v, mask, part, lse, normed, weight_half, tokens, gmid, gain, small, db1, gmixed,
             dfc1, dfc2, dproj, clip_size):
    clips, slots, width = tokens.shape
    rows = gmid.shape[1]
    half = width // 2
    keys = k.shape[1]
    pairs = HEADS // 4
    lanes = 2 * DH
    bits = clip_size.bit_length() - 1
    hidden = db1.shape[1]
    arrays = sum_arrays(width, hidden, clip_size)
    places = step_places(clips, pairs)
    one = pl.Buffered(buffer_count=1)

    def of_pair(s):
        at = jnp.minimum(attention_index(s, places), 2 * clips * pairs - 1)
        return at // (2 * pairs), (at // pairs) % 2, at % pairs

    def of_keys(s):
        clip, _, pair = of_pair(s)
        return clip, 0, pair

    def of_projection(s):
        index = s * 0
        for at in places["projections"][:-1]:
            index = index + (s > at).astype(jnp.int32)
        return index, 0, 0

    def of_clip(s):
        return jnp.clip(s - places["inputs"], 0, clips - 1), 0, 0

    fixed = lambda shape: pl.BlockSpec(shape, lambda s: (0,) * len(shape), pipeline_mode=one)
    tok_pair = pl.BlockSpec((1, rows, lanes), of_pair)
    key_pair = pl.BlockSpec((1, keys, lanes), of_keys)
    anywhere = pl.BlockSpec(memory_space=pl.ANY)
    blocks = (2,) * bits
    r_fc1, r_fc2 = width // clip_size, hidden // clip_size
    dfc1 = dfc1.reshape((2,) + blocks + (r_fc1, hidden // 2))
    dfc2 = dfc2.reshape((2,) + blocks + (r_fc2, half))
    dproj = dproj.reshape((2,) + blocks + (r_fc1, half))
    vmem = lambda *shape: pltpu.VMEM(shape, bf16)
    wide = lambda *shape: pltpu.VMEM(shape, f32)
    scratch = [
        vmem(2, clips, rows, half),
        vmem(clips, 2 * rows, 3 * half),
        wide(pairs, 2, keys, lanes),
        vmem(pairs, 2, 2 * rows, lanes),
        vmem(clips, pairs, 2, 2 * rows, lanes),
        wide(clips, rows, width),
        vmem(clips, rows, width),
        vmem(clips, rows, width),
        wide(width, 3 * half),
        wide(8, half),
        wide(bits + 3, 16, width),
        wide(bits + 2, 16, width),
        vmem(*blocks, r_fc1, hidden // 4),
        vmem(*blocks, r_fc2 // 2, half),
        vmem(*blocks, r_fc1, half),
    ]
    scratch += [vmem(2, *blocks, r, w) for name, _, r, w, _ in arrays if name == "qkv"]
    for _, _, r, w, _ in arrays:
        scratch += [vmem(*((2,) * (bits - stage)), r, w) for stage in range(bits + 1)]
    scratch += [vmem(r, w) for name, _, r, w, _ in arrays if name != "qkv"]
    scratch += [vmem(2, 2, r, w) if name == "qkv" else vmem(2, r, w) for name, _, r, w, _ in arrays]
    dma = lambda *shape: pltpu.SemaphoreType.DMA(shape)
    count = len(arrays)
    scratch += [
        dma(clips), dma(clips), dma(clips), dma(clips, pairs), dma(clips, pairs), dma(clips), dma(clips),
        dma(count, bits + 3), dma(count, bits + 3), dma(count), dma(bits + 2), dma(bits + 2),
    ]
    shape = jax.ShapeDtypeStruct
    return pl.pallas_call(
        functools.partial(backward_kernel, (clips, slots, rows, bits, pairs, arrays)),
        grid=(places["end"] + 1,),
        in_specs=[
            tok_pair, key_pair, key_pair,
            pl.BlockSpec((1, 1, keys), lambda s: (of_pair(s)[0], 0, 0)),
            tok_pair, tok_pair,
            pl.BlockSpec((1, 2 * rows, width), of_projection),
            fixed(weight_half.shape),
            pl.BlockSpec((1, slots, width), of_clip),
            pl.BlockSpec((1, rows, width), of_clip),
            fixed((width,)), fixed((8, width)), fixed((1, hidden)),
            anywhere, anywhere, anywhere, anywhere,
        ],
        out_specs=[
            pl.BlockSpec((1, slots, width), of_clip),
            fixed((r_fc1, hidden)), fixed((r_fc2, width)), fixed((r_fc1, width)),
            fixed((r_fc1, 3 * width)), fixed((16, width)),
        ],
        out_shape=[
            shape((clips, slots, width), f32),
            shape((r_fc1, hidden), bf16),
            shape((r_fc2, width), bf16),
            shape((r_fc1, width), bf16),
            shape((r_fc1, 3 * width), bf16),
            shape((16, width), f32),
        ],
        scratch_shapes=scratch,
        compiler_params=params(collective_id=1, has_side_effects=True),
        cost_estimate=pl.CostEstimate(
            flops=2 * clips * rows * (5 * keys * width + 6 * width * width),
            bytes_accessed=60_000_000,
            transcendentals=clips * rows * keys * HEADS,
        ),
        name="backward",
    )(q, k, v, mask, part, lse, normed, weight_half, tokens, gmid, gain, small, db1, gmixed, dfc1, dfc2, dproj)


def outputs_kernel(fc1, fc2, proj, qkv, vec, gtok, fc1_out, fc2_out, proj_out, qkv_out, gtok_out, db1_out, *rest):
    outs, sem = rest[:-1], rest[-1]
    copy = pltpu.make_async_copy(gtok, gtok_out, sem)
    copy.start()
    for src, dst in ((fc1, fc1_out), (fc2, fc2_out), (proj, proj_out), (qkv, qkv_out)):
        dst[...] = src[...].astype(f32)
    width = vec.shape[1]
    for i, dst in enumerate(outs):
        dst[...] = vec[i : i + 1].reshape(width)
    tall = db1_out.shape[0] // width
    db1_out[...] = jnp.concatenate([vec[8 + i : 9 + i] for i in range(tall)], axis=1).reshape(db1_out.shape[0])
    copy.wait()


def final_outputs(low_fc1, low_fc2, low_proj, low_qkv, summed, gtok, hidden):
    width = summed.shape[1]
    vmem = pl.BlockSpec(memory_space=pltpu.VMEM)
    anywhere = pl.BlockSpec(memory_space=pl.ANY)
    shape = jax.ShapeDtypeStruct
    return pl.pallas_call(
        outputs_kernel,
        in_specs=[vmem] * 5 + [anywhere],
        out_specs=[vmem] * 4 + [anywhere] + [vmem] * 9,
        out_shape=[shape(a.shape, f32) for a in (low_fc1, low_fc2, low_proj, low_qkv)]
        + [shape(gtok.shape, f32), shape((hidden,), f32)]
        + [shape((width,), f32)] * 8,
        scratch_shapes=[pltpu.SemaphoreType.DMA(())],
        compiler_params=params(),
        name="final_outputs",
    )(low_fc1, low_fc2, low_proj, low_qkv, summed, gtok)


def partner(kind):
    index = lax.axis_index("freq")
    if kind == "vert":
        return {"freq": (index + 2) % 4}
    return {"freq": index + 1 - 2 * (index % 2)}


def whole_forward_kernel(
    counts,
    tok_ref, qkv_ref, qb_ref, vb_ref, gain_ref, shift_ref, proj_ref, pb_ref, gain2_ref, shift2_ref,
    q_ref, k_ref, v_ref, normed_ref, mixed_ref, lse_ref, middle_ref, normed2_ref, mask_ref,
    held, send_sem, recv_sem,
):
    clips, slots, rows = counts
    clip = pl.program_id(0)
    pair = pl.program_id(1)
    width = tok_ref.shape[-1]

    def copy(kind, index):
        at = {"vert": 0, "core": 1, "diag": 2}[kind]
        return pltpu.make_async_remote_copy(
            src_ref=held.at[index, 0] if kind == "diag" else tok_ref.at[index],
            dst_ref=held.at[index, at],
            send_sem=send_sem.at[index, at],
            recv_sem=recv_sem.at[index, at],
            device_id=partner(kind),
            device_id_type=pl.DeviceIdType.MESH,
        )

    def project(slot, source):
        unit, _ = center_scale(source.astype(f32))
        normed = (unit * gain_ref[...] + shift_ref[...]).astype(bf16)
        if slot == 0:
            normed_ref[0] = normed
            query = (dot(normed, qkv_ref[:, :width]) + qb_ref[...]).astype(bf16)
            q_ref[0] = query * jnp.asarray(DH ** -0.5, bf16)
        both = dot(normed, qkv_ref[:, width:])
        k_ref[0, slot * rows : (slot + 1) * rows] = both[:, :width].astype(bf16)
        v_ref[0, slot * rows : (slot + 1) * rows] = (both[:, width:] + vb_ref[...]).astype(bf16)
        first = (slots // 16) * 16
        kept = source[first:].astype(f32)[slots - first : slots - first + 1, 0:1] + slots // 2
        lane = lax.broadcasted_iota(jnp.int32, (1, rows), 1).astype(f32)
        return (lane < kept).astype(f32)

    @pl.when((clip == 0) & (pair == 0))
    def enter():
        barrier = pltpu.get_barrier_semaphore()
        for kind in ("vert", "core"):
            pl.semaphore_signal(
                barrier, inc=1, device_id=partner(kind), device_id_type=pl.DeviceIdType.MESH
            )
        pl.semaphore_wait(barrier, 2)
        copy("vert", 0).start()
        for index in range(clips):
            copy("core", index).start()

    def pass_on(index):
        copy("vert", index).wait_recv()
        copy("diag", index).start()
        copy("vert", index).wait_send()

        @pl.when(index + 1 < clips)
        def more():
            copy("vert", index + 1).start()

    @pl.when(pair == 0)
    def project_all():
        live_own = project(0, tok_ref[clip])
        copy("core", clip).wait_recv()
        live_core = project(2, held[clip, 1])

        @pl.when(clip == 0)
        def first_pass():
            pass_on(clip)

        live_vert = project(1, held[clip, 0])
        copy("diag", clip).wait_recv()
        live_diag = project(3, held[clip, 2])
        mask_ref[0] = jnp.concatenate([live_own, live_vert, live_core, live_diag], axis=1)

    @pl.when((pair == 3) & (clip + 1 < clips))
    def next_pass():
        pass_on(clip + 1)

    lanes = pl.ds(pl.multiple_of(pair * 2 * DH, 2 * DH), 2 * DH)
    query = q_ref[0, :, lanes]
    keys = k_ref[0, :, lanes]
    values = v_ref[0, :, lanes]
    live = mask_ref[0] > 0.5
    outs, lses = [], []
    for head in range(2):
        scores = jnp.where(live, dot(only(query, head), keys, NT), MASKED)
        top = jnp.max(scores, axis=1, keepdims=True)
        exps = jnp.exp(scores - top)
        total = jnp.sum(exps, axis=1, keepdims=True)
        outs.append(dot(exps.astype(bf16), values) / total)
        lses.append(top + jnp.log(total))
    first = own_lanes(outs[0].shape, 0)
    mixed_ref[0, :, lanes] = jnp.where(first, outs[0], outs[1]).astype(bf16)
    lse_ref[0, :, lanes] = jnp.where(first, lses[0], lses[1])

    @pl.when(pair == pl.num_programs(1) - 1)
    def finish():
        middle = tok_ref[clip].astype(f32) + (dot(mixed_ref[0], proj_ref[...]) + pb_ref[...])
        middle_ref[0] = middle
        unit, _ = center_scale(middle)
        normed2_ref[0] = (unit * gain2_ref[...] + shift2_ref[...]).astype(bf16)
        copy("core", clip).wait_send()
        copy("diag", clip).wait_send()


def whole_forward(tok, slots, qkv_weight, vectors, proj_weight):
    clips, rows, width = tok.shape
    keys = 4 * rows
    pairs = HEADS // 2
    query_bias, value_bias, gain, shift, proj_bias, gain2, shift2 = vectors
    one = pl.Buffered(buffer_count=1)
    row = full((1, width))
    block = lambda n: pl.BlockSpec((1, n, width), lambda c, p: (c, 0, 0))
    flops = 2 * clips * (10 * rows * width * width + 2 * rows * keys * width)
    weight = lambda w: pl.BlockSpec(w.shape, lambda c, p: (0, 0), pipeline_mode=one)
    return pl.pallas_call(
        functools.partial(whole_forward_kernel, (clips, slots, rows)),
        grid=(clips, pairs),
        in_specs=[
            pl.BlockSpec(tok.shape, lambda c, p: (0, 0, 0), pipeline_mode=one),
            weight(qkv_weight), row, row, row, row, weight(proj_weight), row, row, row,
        ],
        out_specs=[block(rows), block(keys), block(keys)] + [block(rows)] * 5
        + [pl.BlockSpec((1, 1, keys), lambda c, p: (c, 0, 0))],
        out_shape=[
            jax.ShapeDtypeStruct((clips, rows, width), bf16),
            jax.ShapeDtypeStruct((clips, keys, width), bf16),
            jax.ShapeDtypeStruct((clips, keys, width), bf16),
            jax.ShapeDtypeStruct((clips, rows, width), bf16),
            jax.ShapeDtypeStruct((clips, rows, width), bf16),
            jax.ShapeDtypeStruct((clips, rows, width), f32),
            jax.ShapeDtypeStruct((clips, rows, width), f32),
            jax.ShapeDtypeStruct((clips, rows, width), bf16),
            jax.ShapeDtypeStruct((clips, 1, keys), f32),
        ],
        scratch_shapes=[
            pltpu.VMEM((clips, 3, rows, width), bf16),
            pltpu.SemaphoreType.DMA((clips, 3)),
            pltpu.SemaphoreType.DMA((clips, 3)),
        ],
        compiler_params=params(collective_id=0, has_side_effects=True),
        cost_estimate=pl.CostEstimate(
            flops=flops, bytes_accessed=40_000_000, transcendentals=clips * rows * keys * HEADS
        ),
        name="whole_forward",
    )(tok, qkv_weight, query_bias, value_bias, gain, shift, proj_weight, proj_bias, gain2, shift2)


def attend_back_kernel(q_ref, k_ref, v_ref, mask_ref, mixed_ref, lse_ref, grad_ref,
                       dq_ref, dkeep_ref, dsend_ref):
    query = q_ref[0]
    keys = k_ref[0]
    values = v_ref[0]
    grad = grad_ref[0]
    live = mask_ref[0] > 0.5
    product = grad.astype(f32) * mixed_ref[0].astype(f32)
    dqs, dk, dv = [], None, None
    for head in range(2):
        own_query = only(query, head)
        own_grad = only(grad, head)
        scores = jnp.where(live, dot(own_query, keys, NT), MASKED)
        probs = jnp.exp(scores - lse_ref[0, :, head * DH : head * DH + 1])
        delta = jnp.sum(only(product, head), axis=1, keepdims=True)
        dscores = (probs * (dot(own_grad, values, NT) - delta)).astype(bf16)
        dqs.append(dot(dscores, keys))
        more_k = dot(dscores, own_query, TN)
        more_v = dot(probs.astype(bf16), own_grad, TN)
        dk = more_k if dk is None else dk + more_k
        dv = more_v if dv is None else dv + more_v
    first = own_lanes(dqs[0].shape, 0)
    dq_ref[0] = (jnp.where(first, dqs[0], dqs[1]) * DH ** -0.5).astype(bf16)
    half = dk.shape[0] // 2
    dkeep_ref[0, 0] = dk[:half].astype(bf16)
    dkeep_ref[1, 0] = dv[:half].astype(bf16)
    dsend_ref[0, 0] = dk[half:].astype(bf16)
    dsend_ref[1, 0] = dv[half:].astype(bf16)


def attend_back(q, k, v, mask, mixed, lse, grad, first_pair, pairs):
    clips, rows, _ = q.shape
    keys = k.shape[1]
    lanes = 2 * DH
    tok = pl.BlockSpec((1, rows, lanes), lambda c, p: (c, 0, first_pair + p))
    key = pl.BlockSpec((1, keys, lanes), lambda c, p: (c, 0, first_pair + p))
    part = pl.BlockSpec((2, 1, keys // 2, lanes), lambda c, p: (0, c, 0, p))
    return pl.pallas_call(
        attend_back_kernel,
        grid=(clips, pairs),
        in_specs=[tok, key, key, pl.BlockSpec((1, 1, keys), lambda c, p: (c, 0, 0)), tok, tok, tok],
        out_specs=[pl.BlockSpec((1, rows, lanes), lambda c, p: (c, 0, p)), part, part],
        out_shape=[
            jax.ShapeDtypeStruct((clips, rows, pairs * lanes), bf16),
            jax.ShapeDtypeStruct((2, clips, keys // 2, pairs * lanes), bf16),
            jax.ShapeDtypeStruct((2, clips, keys // 2, pairs * lanes), bf16),
        ],
        compiler_params=params(),
        cost_estimate=pl.CostEstimate(
            flops=4 * 10 * clips * rows * keys * pairs * lanes,
            bytes_accessed=clips * pairs * lanes * (keys * 10 + rows * 12),
            transcendentals=clips * rows * keys * 2 * pairs,
        ),
        name="attend_back",
    )(q, k, v, mask, mixed, lse, grad)


def weight_kernel(normed_ref, dq_ref, dk0_ref, dk1_ref, dk2_ref, out_ref, dkv_ref, sums_ref):
    part = pl.program_id(0)
    @pl.when(part == 0)
    def query():
        grad = dq_ref[...]
        out_ref[0] = dot(normed_ref[...], grad, TN).astype(bf16)
        sums_ref[0] = column_sums(grad.astype(f32))
        dkv_ref[0] = jnp.zeros_like(dkv_ref[0])

    @pl.when(part > 0)
    def other():
        grad = (dk0_ref[0].astype(f32) + dk1_ref[0].astype(f32) + dk2_ref[0].astype(f32)).astype(bf16)
        dkv_ref[0] = grad
        out_ref[0] = dot(normed_ref[...], grad, TN).astype(bf16)
        sums_ref[0] = column_sums(grad.astype(f32))


def weight_grads(normed, dq, parts):
    total, width = normed.shape
    lanes = dq.shape[1]
    before = lambda j: (jnp.maximum(j - 1, 0), 0, 0)
    part = pl.BlockSpec((1, total, lanes), before)
    return pl.pallas_call(
        weight_kernel,
        grid=(3,),
        in_specs=[full((total, width)), full((total, lanes)), part, part, part],
        out_specs=[
            pl.BlockSpec((1, width, lanes), lambda j: (j, 0, 0)),
            part,
            pl.BlockSpec((1, 1, lanes), lambda j: (j, 0, 0)),
        ],
        out_shape=[
            jax.ShapeDtypeStruct((3, width, lanes), bf16),
            jax.ShapeDtypeStruct((2, total, lanes), bf16),
            jax.ShapeDtypeStruct((3, 1, lanes), f32),
        ],
        compiler_params=params(),
        cost_estimate=pl.CostEstimate(
            flops=6 * total * width * lanes, bytes_accessed=8_000_000, transcendentals=0
        ),
        name="weight_grads",
    )(normed, dq, *parts)


def input_kernel(counts, groups, *refs):
    clips, slots, rows = counts
    dqs = refs[:groups]
    dkvs = refs[groups : 2 * groups]
    qkv_ref, tok_ref, gmid_ref, gain_ref, shift_ref, out_ref, small_ref = refs[2 * groups :]
    clip = pl.program_id(0)
    width = tok_ref.shape[-1]
    lanes = width // groups
    grad = None
    for group in range(groups):
        for part in range(3):
            rows_grad = dqs[group][0] if part == 0 else dkvs[group][part - 1]
            at = part * width + group * lanes
            more = dot(rows_grad, qkv_ref[:, at : at + lanes], NT)
            grad = more if grad is None else grad + more
    unit, inverse = center_scale(tok_ref[0].astype(f32))
    result = gmid_ref[0] + norm_back(unit, inverse, gain_ref[...], grad)
    out_ref[0] = result[:slots]

    @pl.when(clip == 0)
    def start():
        small_ref[...] = jnp.zeros_like(small_ref)

    small_ref[0:1] += column_sums(grad * unit)
    small_ref[1:2] += column_sums(grad)


def input_grads(dqs, dkvs, qkv_weight, tokens, gmid, gain, shift, slots):
    clips, rows, width = tokens.shape
    groups = len(dqs)
    lanes = width // groups
    tok = pl.BlockSpec((1, rows, width), lambda c: (c, 0, 0))
    return pl.pallas_call(
        functools.partial(input_kernel, (clips, slots, rows), groups),
        grid=(clips,),
        in_specs=[pl.BlockSpec((1, rows, lanes), lambda c: (c, 0, 0))] * groups
        + [pl.BlockSpec((2, rows, lanes), lambda c: (0, c, 0))] * groups
        + [full(qkv_weight.shape), tok, tok, full((1, width)), full((1, width))],
        out_specs=[pl.BlockSpec((1, slots, width), lambda c: (c, 0, 0)), full((8, width))],
        out_shape=[
            jax.ShapeDtypeStruct((clips, slots, width), f32),
            jax.ShapeDtypeStruct((8, width), f32),
        ],
        compiler_params=params(),
        cost_estimate=pl.CostEstimate(
            flops=6 * clips * rows * width * width, bytes_accessed=16_000_000, transcendentals=0
        ),
        name="input_grads",
    )(*dqs, *dkvs, qkv_weight, tokens, gmid, gain, shift)


def swap_bit(array, axis, size, bit):
    return lax.ppermute(array, axis, [(i, i ^ (1 << bit)) for i in range(size)])


def add_low(left, right):
    return (left.astype(f32) + right.astype(f32)).astype(bf16)


def pick(array, index, dim):
    return lax.dynamic_index_in_dim(array, index, dim, keepdims=False)


def bit_of(axis, bit):
    return (lax.axis_index(axis) >> bit) & 1


def scatter_sum(split, clip_size, order):
    core = bit_of("freq", 0)
    vert = bit_of("freq", 1)
    bits = clip_size.bit_length() - 1
    lanes = split.shape[-1]
    value = add_low(pick(split, core, 0), swap_bit(pick(split, 1 - core, 0), "freq", 4, 0))
    rows = value.shape[0] // (2 * clip_size)
    value = value.reshape((2,) * bits + (2, rows, lanes))
    left = list(range(bits))[::-1]
    for bit in order:
        at = left.index(bit)
        mine = bit_of("clip", bit)
        value = add_low(
            pick(value, mine, at), swap_bit(pick(value, 1 - mine, at), "clip", clip_size, bit)
        )
        left.remove(bit)
    return add_low(pick(value, vert, 0), swap_bit(pick(value, 1 - vert, 0), "freq", 4, 1))


def gather_low(part):
    core = bit_of("freq", 0)
    vert = bit_of("freq", 1)
    other = swap_bit(part, "freq", 4, 1)
    tall = jnp.where(vert == 0, jnp.concatenate([part, other]), jnp.concatenate([other, part]))
    side = swap_bit(tall, "freq", 4, 0)
    return jnp.where(
        core == 0,
        jnp.concatenate([tall, side], axis=1),
        jnp.concatenate([side, tall], axis=1),
    ).astype(f32)


def total_sum(array, clip_size):
    for bit in range(2):
        array = array + swap_bit(array, "freq", 4, bit)
    for bit in range(clip_size.bit_length() - 1):
        array = array + swap_bit(array, "clip", clip_size, bit)
    return array


def on_device_plain(
    clip_size, tokens, kept_counts, attn_gain, attn_shift, qkv_weight, query_bias, value_bias,
    proj_weight, proj_bias, mlp_gain, mlp_shift, fc1_weight, fc1_bias, fc2_weight, fc2_bias, cotangent,
):
    clips, slots, width = tokens.shape
    rows = -(-slots // 16) * 16
    total = clips * rows
    bits = clip_size.bit_length() - 1
    forward_order = list(range(bits))
    second_order = forward_order[1:2] + forward_order[:1] + forward_order[2:]
    vec = lambda v: v.astype(f32)[None, :]
    kept = (kept_counts - slots // 2).astype(bf16)
    tok = jnp.concatenate(
        [tokens, jnp.broadcast_to(kept[:, :, None], (clips, rows - slots, width))], axis=1
    )
    vectors = [vec(v) for v in (query_bias, value_bias, attn_gain, attn_shift, proj_bias, mlp_gain, mlp_shift)]
    q, k, v, normed, mixed, lse, middle, normed2, mask = whole_forward(
        tok, slots, qkv_weight, vectors, proj_weight
    )
    flat = lambda a: a.reshape(total, width)
    layer_out, dfc1, dfc2, dproj, db1, small2, gmid, gmixed = mlp(
        kept_counts, flat(normed2), flat(middle), cotangent, flat(mixed), fc1_weight, fc1_bias,
        fc2_weight, fc2_bias, mlp_gain, proj_weight, rows,
    )
    early = total_sum(jnp.concatenate([small2[:4].reshape(-1), db1.reshape(-1)])[None, :], clip_size)[0]
    sum_fc1 = gather_low(scatter_sum(dfc1, clip_size, forward_order))
    sum_fc2 = gather_low(scatter_sum(dfc2, clip_size, second_order))
    sum_proj = gather_low(scatter_sum(dproj, clip_size, forward_order))

    groups = 3
    pairs = HEADS // 2 // groups
    lanes = pairs * 2 * DH
    gmixed = gmixed.reshape(clips, rows, width)
    dqs, dkvs, sums, sharded = [], [], [], []
    for group in range(groups):
        dq, keep, send = attend_back(q, k, v, mask, mixed, lse, gmixed, group * pairs, pairs)
        got = swap_bit(send, "freq", 4, 0)
        across = swap_bit(add_low(keep[:, :, rows:], got[:, :, rows:]), "freq", 4, 1)
        parts = [a.reshape(2, total, lanes) for a in (keep[:, :, :rows], got[:, :, :rows], across)]
        dw, dkv, colsum = weight_grads(flat(normed), dq.reshape(total, lanes), parts)
        half = lanes // 2
        split = jnp.stack(
            [
                jnp.concatenate([dw[i, :, s * half : (s + 1) * half] for i in range(3)], axis=1)
                for s in range(2)
            ]
        )
        order = forward_order if group % 2 == 0 else second_order
        summed = gather_low(scatter_sum(split, clip_size, order))
        sharded.append(summed.reshape(summed.shape[0], 2, 3, half))
        dqs.append(dq)
        dkvs.append(dkv)
        sums.append(colsum)
    grad_tokens, small1 = input_grads(
        dqs, dkvs, qkv_weight, tok, gmid.reshape(clips, rows, width), vectors[2], vectors[3], slots
    )
    qkv = jnp.stack(sharded, axis=1)
    sum_qkv = qkv.transpose(0, 3, 1, 2, 4).reshape(qkv.shape[0], 3 * width)
    bias = jnp.concatenate(sums, axis=2)
    late = total_sum(
        jnp.concatenate([small1[0:1], small1[1:2], bias[0], bias[2]], axis=1), clip_size
    )[0]
    cut = lambda a, i: a[i * width : (i + 1) * width]
    return (
        layer_out, grad_tokens, cut(late, 0), cut(late, 1), sum_qkv, cut(late, 2), cut(late, 3),
        sum_proj, cut(early, 3), cut(early, 0), cut(early, 1), sum_fc1, early[4 * width :],
        sum_fc2, cut(early, 2),
    )


def on_device(
    clip_size, tokens, kept_counts, attn_gain, attn_shift, qkv_weight, query_bias, value_bias,
    proj_weight, proj_bias, mlp_gain, mlp_shift, fc1_weight, fc1_bias, fc2_weight, fc2_bias, cotangent,
):
    clips, slots, width = tokens.shape
    rows = -(-slots // 16) * 16
    if clip_size != 8 or width % (32 * clip_size):
        return on_device_plain(
            clip_size, tokens, kept_counts, attn_gain, attn_shift, qkv_weight, query_bias, value_bias,
            proj_weight, proj_bias, mlp_gain, mlp_shift, fc1_weight, fc1_bias, fc2_weight, fc2_bias, cotangent,
        )
    q, k, v, normed, part, lse, mask, weight_half, mixed, middle, normed2 = forward(
        kept_counts, tokens, rows, qkv_weight, query_bias, value_bias, attn_gain, attn_shift,
        proj_weight, proj_bias, mlp_gain, mlp_shift,
    )
    flat = lambda a: a.reshape(clips * rows, width)
    layer_out, dfc1, dfc2, dproj, db1, small, gmid, gmixed = mlp(
        kept_counts, flat(normed2), flat(middle), cotangent, flat(mixed), fc1_weight, fc1_bias,
        fc2_weight, fc2_bias, mlp_gain, proj_weight, rows,
    )
    by_clip = lambda a: a.reshape(clips, rows, width)
    gtok, low_fc1, low_fc2, low_proj, low_qkv, summed = backward(
        q, k, v, mask, part, lse, normed, weight_half, tokens, by_clip(gmid), attn_gain, small, db1,
        by_clip(gmixed), dfc1, dfc2, dproj, clip_size,
    )
    fc1, fc2, proj, qkv, grad_tokens, fc1_b, *rows_out = final_outputs(
        low_fc1, low_fc2, low_proj, low_qkv, summed, gtok, fc1_bias.shape[0]
    )
    return (
        layer_out, grad_tokens, rows_out[0], rows_out[1], qkv, rows_out[2], rows_out[3], proj, rows_out[7],
        rows_out[4], rows_out[5], fc1, fc1_b, fc2, rows_out[6],
    )


def solution(mesh):
    rows = P("clip", "freq", None)
    shard = P("clip", None)
    return jax.shard_map(
        functools.partial(on_device, mesh.shape["clip"]),
        mesh=mesh,
        in_specs=(rows, P("clip", "freq")) + (P(),) * 13 + (rows,),
        out_specs=(rows, rows, P(), P(), shard, P(), P(), shard, P(), P(), P(), shard, P(), shard, P()),
        check_vma=False,
    )
```

profile of v0, /device:TPU:0, one launch (start us, length us, event | category | flops | bytes accessed | tf_op | source)
XLA Modules:
  0.0 329.2 jit_solution(7895167307287150393)
XLA Ops:
  0.6 1.3 copy.32.kept_ref
  2.0 75.0 %forward.1 = (bf16[3,608,384]{2,1,0:T(8,128)(2,1)}, bf16[3,1216,384]{2,1,0:T(8,128)(2,1)}, bf16[3,1216,384]{2,1,0:T(8,128)(2,1)}, bf16[3,608,768]{2,1,0:T(8,128)...) custom-call(s32[3,1]{1,0:T(4,128)} %copy.32.kept_ref, ...), custom_call_target="tpu_custom_call" | custom-call | flops 9861857280 | bytes 40000000 | tf_op jit(solution)/shard_map/forward/pallas_call | solution.py:246
  77.0 50.9 %mlp.1 = (bf16[3,298,768]{2,1,0:T(8,128)(2,1)}, bf16[2,768,1536]{2,1,0:T(8,128)(2,1)}, bf16[2,3072,384]{2,1,0:T(8,128)(2,1)}, bf16[2,768,384]{2,1,0:T(8,128)(2,1...) custom-call(s32[3,1]{1,0:T(4,128)} %copy.32.kept_ref, ...), custom_call_target="tpu_custom_call" | custom-call | flops 25820135424 | bytes 40000000 | tf_op jit(solution)/shard_map/mlp/pallas_call | solution.py:392
  127.8 111.9 %backward.1 = (f32[3,298,768]{2,1,0:T(8,128)}, bf16[96,3072]{1,0:T(8,128)(2,1)}, bf16[384,768]{1,0:T(8,128)(2,1)}, bf16[96,768]{1,0:T(8,128)(2,1)}, bf16[96,2304]{1,0:T(8,128)(2,1)}, /*index=5*/f32[16,768]{1,0:T(8,128)}) custom-call(bf16[3,608,384]{2,1,0:T(8,128)(2,1)} %get-tuple-element.58.q_ref, bf16[3,1216,384]{2,1,0:T(8,128)(2,1)} %get-tuple-element.59.k_ref, ...), custom_call_target="tpu_custom_call" | custom-call | flops 14972092416 | bytes 60000000 | tf_op jit(solution)/shard_map/backward/pallas_call | solution.py:887
  239.8 89.2 %final_outputs.1 = (f32[96,3072]{1,0:T(8,128)}, f32[384,768]{1,0:T(8,128)}, f32[96,768]{1,0:T(8,128)}, f32[96,2304]{1,0:T(8,128)}, f32[3,298,768]{2,1,0:T(8,128)...) custom-call(bf16[96,3072]{1,0:T(8,128)(2,1)} %get-tuple-element.73.f, ...), custom_call_target="tpu_custom_call" | custom-call | tf_op jit(solution)/shard_map/final_outputs/pallas_call | solution.py:944
where the time goes:
time: 329 us
  Pallas kernels  327 us (99%)
    pallas_call x1, Pallas kernels, backward(): pl.pallas_call(functools.partial(backward_kernel, (clips, slots, rows, bi...  112 us
    pallas_call x1, Pallas kernels, final_outputs(): pl.pallas_call(outputs_kernel, in_specs=[vmem] * 5 + [anywhere], out_spec...  89.2 us
    pallas_call x1, Pallas kernels, forward(): pl.pallas_call(functools.partial(forward_kernel, (clips, slots, rows, pai...  75 us
    pallas_call x1, Pallas kernels, mlp(): pl.pallas_call(functools.partial(mlp_kernel, (clips, slots, rows, tile)),...  50.9 us

commit v1 on v0

--- a/solution.py
+++ b/solution.py
@@ -922,36 +922,38 @@
     )(q, k, v, mask, part, lse, normed, weight_half, tokens, gmid, gain, small, db1, gmixed, dfc1, dfc2, dproj)
 
 
-def outputs_kernel(fc1, fc2, proj, qkv, vec, gtok, fc1_out, fc2_out, proj_out, qkv_out, gtok_out, db1_out, *rest):
-    outs, sem = rest[:-1], rest[-1]
-    copy = pltpu.make_async_copy(gtok, gtok_out, sem)
-    copy.start()
-    for src, dst in ((fc1, fc1_out), (fc2, fc2_out), (proj, proj_out), (qkv, qkv_out)):
-        dst[...] = src[...].astype(f32)
-    width = vec.shape[1]
-    for i, dst in enumerate(outs):
-        dst[...] = vec[i : i + 1].reshape(width)
-    tall = db1_out.shape[0] // width
-    db1_out[...] = jnp.concatenate([vec[8 + i : 9 + i] for i in range(tall)], axis=1).reshape(db1_out.shape[0])
-    copy.wait()
+def outputs_kernel(fc1, fc2, proj, qkv, vec, gtok, fc1_out, fc2_out, proj_out, qkv_out, gtok_out, db1_out, *outs):
+    gtok_out[...] = gtok[...]
+
+    @pl.when(pl.program_id(0) == 0)
+    def others():
+        for src, dst in ((fc1, fc1_out), (fc2, fc2_out), (proj, proj_out), (qkv, qkv_out)):
+            dst[...] = src[...].astype(f32)
+        width = vec.shape[1]
+        for i, dst in enumerate(outs):
+            dst[...] = vec[i : i + 1].reshape(width)
+        tall = db1_out.shape[0] // width
+        db1_out[...] = jnp.concatenate([vec[8 + i : 9 + i] for i in range(tall)], axis=1).reshape(db1_out.shape[0])
 
 
 def final_outputs(low_fc1, low_fc2, low_proj, low_qkv, summed, gtok, hidden):
     width = summed.shape[1]
-    vmem = pl.BlockSpec(memory_space=pltpu.VMEM)
-    anywhere = pl.BlockSpec(memory_space=pl.ANY)
+    one = pl.Buffered(buffer_count=1)
+    fixed = lambda shape: pl.BlockSpec(shape, lambda c: (0,) * len(shape), pipeline_mode=one)
+    by_clip = pl.BlockSpec((1,) + gtok.shape[1:], lambda c: (c, 0, 0))
     shape = jax.ShapeDtypeStruct
+    lows = (low_fc1, low_fc2, low_proj, low_qkv)
     return pl.pallas_call(
         outputs_kernel,
-        in_specs=[vmem] * 5 + [anywhere],
-        out_specs=[vmem] * 4 + [anywhere] + [vmem] * 9,
-        out_shape=[shape(a.shape, f32) for a in (low_fc1, low_fc2, low_proj, low_qkv)]
+        grid=(gtok.shape[0],),
+        in_specs=[fixed(a.shape) for a in lows] + [fixed(summed.shape), by_clip],
+        out_specs=[fixed(a.shape) for a in lows] + [by_clip, fixed((hidden,))] + [fixed((width,))] * 8,
+        out_shape=[shape(a.shape, f32) for a in lows]
         + [shape(gtok.shape, f32), shape((hidden,), f32)]
         + [shape((width,), f32)] * 8,
-        scratch_shapes=[pltpu.SemaphoreType.DMA(())],
         compiler_params=params(),
         name="final_outputs",
-    )(low_fc1, low_fc2, low_proj, low_qkv, summed, gtok)
+    )(*lows, summed, gtok)
 
 
 def partner(kind):

time: 329 us -> 246 us (0.75)
  Pallas kernels: 327 us -> 244 us
    pallas_call x1, Pallas kernels: 89.2 us -> 6.1 us  [final_outputs(): pl.pallas_call(outputs_kernel, grid=(gtok.shape[0],), in_specs=[fixed(a.s...]
where the time goes in v1:
time: 246 us
  Pallas kernels  244 us (99%)
    pallas_call x1, Pallas kernels, backward(): pl.pallas_call(functools.partial(backward_kernel, (clips, slots, rows, bi...  112 us
    pallas_call x1, Pallas kernels, forward(): pl.pallas_call(functools.partial(forward_kernel, (clips, slots, rows, pai...  75 us
    pallas_call x1, Pallas kernels, mlp(): pl.pallas_call(functools.partial(mlp_kernel, (clips, slots, rows, tile)),...  50.9 us
    pallas_call x1, Pallas kernels, final_outputs(): pl.pallas_call(outputs_kernel, grid=(gtok.shape[0],), in_specs=[fixed(a.s...  6.1 us

profile of v1, /device:TPU:0, one launch (start us, length us, event | category | flops | bytes accessed | tf_op | source)
XLA Modules:
  0.0 246.0 jit_solution(14182179337134042626)
XLA Ops:
  0.6 1.3 copy.32.kept_ref
  2.0 75.0 %forward.1 = (bf16[3,608,384]{2,1,0:T(8,128)(2,1)}, bf16[3,1216,384]{2,1,0:T(8,128)(2,1)}, bf16[3,1216,384]{2,1,0:T(8,128)(2,1)}, bf16[3,608,768]{2,1,0:T(8,128)...) custom-call(s32[3,1]{1,0:T(4,128)} %copy.32.kept_ref, ...), custom_call_target="tpu_custom_call" | custom-call | flops 9861857280 | bytes 40000000 | tf_op jit(solution)/shard_map/forward/pallas_call | solution.py:246
  77.0 50.9 %mlp.1 = (bf16[3,298,768]{2,1,0:T(8,128)(2,1)}, bf16[2,768,1536]{2,1,0:T(8,128)(2,1)}, bf16[2,3072,384]{2,1,0:T(8,128)(2,1)}, bf16[2,768,384]{2,1,0:T(8,128)(2,1...) custom-call(s32[3,1]{1,0:T(4,128)} %copy.32.kept_ref, ...), custom_call_target="tpu_custom_call" | custom-call | flops 25820135424 | bytes 40000000 | tf_op jit(solution)/shard_map/mlp/pallas_call | solution.py:392
  127.8 111.9 %backward.1 = (f32[3,298,768]{2,1,0:T(8,128)}, bf16[96,3072]{1,0:T(8,128)(2,1)}, bf16[384,768]{1,0:T(8,128)(2,1)}, bf16[96,768]{1,0:T(8,128)(2,1)}, bf16[96,2304]{1,0:T(8,128)(2,1)}, /*index=5*/f32[16,768]{1,0:T(8,128)}) custom-call(bf16[3,608,384]{2,1,0:T(8,128)(2,1)} %get-tuple-element.58.q_ref, bf16[3,1216,384]{2,1,0:T(8,128)(2,1)} %get-tuple-element.59.k_ref, ...), custom_call_target="tpu_custom_call" | custom-call | flops 14972092416 | bytes 60000000 | tf_op jit(solution)/shard_map/backward/pallas_call | solution.py:887
  239.8 6.1 %final_outputs.1 = (f32[96,3072]{1,0:T(8,128)}, f32[384,768]{1,0:T(8,128)}, f32[96,768]{1,0:T(8,128)}, f32[96,2304]{1,0:T(8,128)}, f32[3,298,768]{2,1,0:T(8,128)...) custom-call(bf16[96,3072]{1,0:T(8,128)(2,1)} %get-tuple-element.73.f, ...), custom_call_target="tpu_custom_call" | custom-call | tf_op jit(solution)/shard_map/final_outputs/pallas_call | solution.py:946

commit v2 on v1

--- a/solution.py
+++ b/solution.py
@@ -78,12 +78,14 @@
 def forward_kernel(
     counts,
     kept_ref, tok_ref, qkv_ref, qb_ref, vb_ref, gain_ref, shift_ref, proj_ref, pb_ref, gain2_ref, shift2_ref,
-    q_ref, k_ref, v_ref, normed_ref, part_ref, lse_ref, mask_ref, weight_ref, mixed_ref, middle_ref, normed2_ref,
-    own, held, mix_send, mix_got, vecs, tok_send, tok_recv, part_send, part_recv,
+    q_out, k_out, v_out, normed_out, weight_out, part_ref, lse_ref, mask_ref, mixed_ref, middle_ref, normed2_ref,
+    q_all, k_all, v_all, normed_all, weight, live_all, own, held, mix_send, mix_got, own_mix, vecs,
+    tok_send, tok_recv, part_send, part_recv, out_sem, weight_sem,
 ):
     clips, slots, rows, pairs = counts
     clip = pl.program_id(0)
-    pair = pl.program_id(1)
+    turn = pl.program_id(1)
+    slot = 1 - turn
     width = tok_ref.shape[-1]
     half = width // 2
     lanes = 2 * DH
@@ -111,32 +113,34 @@
             device_id_type=mesh_id,
         )
 
-    def project(slot, source):
+    def project(index, slot, source):
         unit, _ = center_scale(source.astype(f32))
         normed = (unit * vecs[2:3] + vecs[3:4]).astype(bf16)
         at = slice(slot * rows, (slot + 1) * rows)
         if slot < 2:
-            normed_ref[0, at] = normed
-            query = (dot(normed, weight_ref[:, :half]) + vecs[0:1, lane_slice(vert * half, half)]).astype(bf16)
-            q_ref[0, at] = query * jnp.asarray(DH ** -0.5, bf16)
-        both = dot(normed, weight_ref[:, half:])
-        k_ref[0, at] = both[:, :half].astype(bf16)
-        v_ref[0, at] = (both[:, half:] + vecs[1:2, lane_slice(vert * half, half)]).astype(bf16)
+            normed_all[index, at] = normed
+            query = (dot(normed, weight[:, :half]) + vecs[0:1, lane_slice(vert * half, half)]).astype(bf16)
+            q_all[index, at] = query * jnp.asarray(DH ** -0.5, bf16)
+        both = dot(normed, weight[:, half:])
+        k_all[index, at] = both[:, :half].astype(bf16)
+        v_all[index, at] = (both[:, half:] + vecs[1:2, lane_slice(vert * half, half)]).astype(bf16)
         first = (slots // 16) * 16
         kept = source[first:].astype(f32)[slots - first : slots - first + 1, 0:1] + slots // 2
         lane = lax.broadcasted_iota(jnp.int32, (1, rows), 1).astype(f32)
-        return (lane < kept).astype(f32)
-
-    def pass_on(index):
-        copy("vert", index).wait_recv()
-        copy("diag", index).start()
-        copy("vert", index).wait_send()
-
-        @pl.when(index + 1 < clips)
-        def more():
-            copy("vert", index + 1).start()
-
-    @pl.when((clip == 0) & (pair == 0))
+        live_all[index, slot] = (lane < kept).astype(f32)
+
+    def out_copies(index):
+        return [
+            pltpu.make_async_copy(src.at[index], dst.at[index], out_sem.at[index, i])
+            for i, (src, dst) in enumerate(
+                ((q_all, q_out), (k_all, k_out), (v_all, v_out), (normed_all, normed_out))
+            )
+        ]
+
+    def weight_copy():
+        return pltpu.make_async_copy(weight, weight_out, weight_sem)
+
+    @pl.when((clip == 0) & (turn == 0))
     def enter():
         barrier = pltpu.get_barrier_semaphore()
         for device in (vert_dev, core_dev):
@@ -153,30 +157,45 @@
         for i, ref in enumerate((qb_ref, vb_ref, gain_ref, shift_ref, pb_ref, gain2_ref, shift2_ref)):
             vecs[i : i + 1] = row_of(ref)
         for part in range(3):
-            weight_ref[:, part * half : (part + 1) * half] = qkv_ref[:, lane_slice(part * width + vert * half, half)]
-
-    @pl.when(pair == 0)
-    def project_all():
-        live_own = project(0, own[clip])
-        copy("core", clip).wait_recv()
-        live_core = project(2, held[clip, 1])
-
-        @pl.when(clip == 0)
-        def first_pass():
-            pass_on(clip)
-
-        live_vert = project(1, held[clip, 0])
+            weight[:, part * half : (part + 1) * half] = qkv_ref[:, lane_slice(part * width + vert * half, half)]
+        weight_copy().start()
+
+        def own_slots(index, carry):
+            project(index, 0, own[index])
+            return carry
+
+        def core_slots(index, carry):
+            copy("core", index).wait_recv()
+            project(index, 2, held[index, 1])
+            return carry
+
+        lax.fori_loop(0, clips, own_slots, 0)
+        lax.fori_loop(0, clips, core_slots, 0)
+        copy("vert", 0).wait_recv()
+        copy("diag", 0).start()
+        copy("vert", 0).wait_send()
+        if clips > 1:
+            copy("vert", 1).start()
+
+    @pl.when(turn == 0)
+    def project_rest():
+        project(clip, 1, held[clip, 0])
         copy("diag", clip).wait_recv()
-        live_diag = project(3, held[clip, 2])
-        mask_ref[0] = jnp.concatenate([live_own, live_vert, live_core, live_diag], axis=1)
-
-    @pl.when((pair == 1) & (clip + 1 < clips))
-    def next_pass():
-        pass_on(clip + 1)
+        project(clip, 3, held[clip, 2])
+        for i in range(4):
+            mask_ref[0, :, i * rows : (i + 1) * rows] = live_all[clip, i]
+        for move in out_copies(clip):
+            move.start()
+
+    for index in range(2, clips):
+        @pl.when((turn == 1) & (clip == index - 2))
+        def send_ahead(index=index):
+            copy("vert", index - 1).wait_send()
+            copy("vert", index).start()
 
     def finish(index):
         at = lane_slice(vert * half, half)
-        mixed_ref[0, :, at] = mix_own_of(index)
+        mixed_ref[0, :, at] = own_mix[...]
         for which in range(pairs):
             mix_copy(index, which).wait_recv()
             at = lane_slice((1 - vert) * half + which * lanes, lanes)
@@ -190,16 +209,13 @@
         for which in range(pairs):
             mix_copy(index, which).wait_send()
 
-    def mix_own_of(index):
-        return jnp.concatenate([mix_send[index, pairs + which] for which in range(pairs)], axis=1)
-
-    here = lane_slice(pair * lanes, lanes)
-    keys = k_ref[0, :, here]
-    values = v_ref[0, :, here]
+    at = pl.ds(pl.multiple_of(slot * rows, rows), rows)
     live = mask_ref[0] > 0.5
-    for slot in (1, 0):
-        at = slice(slot * rows, (slot + 1) * rows)
-        query = q_ref[0, at, here]
+    for pair in range(pairs):
+        here = slice(pair * lanes, (pair + 1) * lanes)
+        keys = k_all[clip, :, here]
+        values = v_all[clip, :, here]
+        query = q_all[clip, at, here]
         outs, lses = [], []
         for head in range(2):
             scores = jnp.where(live, dot(only(query, head), keys, NT), MASKED)
@@ -212,19 +228,37 @@
         mixed = jnp.where(first, outs[0], outs[1]).astype(bf16)
         part_ref[0, at, here] = mixed
         lse_ref[0, at, here] = jnp.where(first, lses[0], lses[1])
-        if slot == 1:
-            mix_send[clip, pair] = mixed
+
+    @pl.when(slot == 1)
+    def give():
+        for pair in range(pairs):
+            mix_send[clip, pair] = part_ref[0, rows:, pair * lanes : (pair + 1) * lanes]
             mix_copy(clip, pair).start()
-        else:
-            mix_send[clip, pairs + pair] = mixed
-
-    last = pairs - 1
-    for index in range(clips):
-        when = (clip == index) & (pair == last) if index == clips - 1 else (clip == index + 1) & (pair == 1)
-
-        @pl.when(when)
-        def finish_clip(index=index):
-            finish(index)
+
+    @pl.when((turn == 0) & (clip > 0))
+    def finish_before():
+        finish(clip - 1)
+
+    @pl.when(turn == 1)
+    def keep_own():
+        own_mix[...] = part_ref[0, :rows]
+
+    @pl.when((turn == 1) & (clip + 1 < clips))
+    def pass_on():
+        copy("vert", clip + 1).wait_recv()
+        copy("diag", clip + 1).start()
+
+    @pl.when((turn == 1) & (clip == clips - 1))
+    def finish_last():
+        finish(clip)
+        copy("vert", clips - 1).wait_send()
+
+    @pl.when((turn == 1) & (clip == clips - 1))
+    def leave():
+        weight_copy().wait()
+        for index in range(clips):
+            for move in out_copies(index):
+                move.wait()
 
 
 def forward(kept, tokens, rows, qkv_weight, query_bias, value_bias, gain, shift, proj_weight, proj_bias, gain2, shift2):
@@ -235,50 +269,56 @@
     lanes = 2 * DH
     one = pl.Buffered(buffer_count=1)
     block = lambda n, m: pl.BlockSpec((1, n, m), lambda c, p: (c, 0, 0))
-    late = lambda n, m: pl.BlockSpec(
-        (1, n, m),
-        lambda c, p: (jnp.where((c == clips - 1) & (p == pairs - 1), c, jnp.maximum(c - 1, 0)), 0, 0),
-    )
+    late = pl.BlockSpec((1, rows, width), lambda c, t: (jnp.maximum(c - 1 + t, 0), 0, 0))
+    anywhere = pl.BlockSpec(memory_space=pl.ANY)
     whole = lambda a: pl.BlockSpec(a.shape, lambda c, p: (0,) * a.ndim, pipeline_mode=one)
     shape = jax.ShapeDtypeStruct
     flops = 2 * clips * (rows * width * width * 6 + 2 * rows * keys * width)
     vectors = (query_bias, value_bias, gain, shift)
     return pl.pallas_call(
         functools.partial(forward_kernel, (clips, slots, rows, pairs)),
-        grid=(clips, pairs),
+        grid=(clips, 2),
         in_specs=[pl.BlockSpec(memory_space=pltpu.SMEM), whole(tokens), whole(qkv_weight)]
         + [whole(v) for v in vectors]
         + [whole(proj_weight)]
         + [whole(v) for v in (proj_bias, gain2, shift2)],
         out_specs=[
-            block(2 * rows, half), block(keys, half), block(keys, half), block(2 * rows, width),
+            anywhere, anywhere, anywhere, anywhere, anywhere,
             block(2 * rows, half), block(2 * rows, half), block(1, keys),
-            pl.BlockSpec((width, 3 * half), lambda c, p: (0, 0), pipeline_mode=one),
-            late(rows, width), late(rows, width), late(rows, width),
+            late, late, late,
         ],
         out_shape=[
             shape((clips, 2 * rows, half), bf16),
             shape((clips, keys, half), bf16),
             shape((clips, keys, half), bf16),
             shape((clips, 2 * rows, width), bf16),
+            shape((width, 3 * half), bf16),
             shape((clips, 2 * rows, half), bf16),
             shape((clips, 2 * rows, half), f32),
             shape((clips, 1, keys), f32),
-            shape((width, 3 * half), bf16),
             shape((clips, rows, width), bf16),
             shape((clips, rows, width), f32),
             shape((clips, rows, width), bf16),
         ],
         scratch_shapes=[
+            pltpu.VMEM((clips, 2 * rows, half), bf16),
+            pltpu.VMEM((clips, keys, half), bf16),
+            pltpu.VMEM((clips, keys, half), bf16),
+            pltpu.VMEM((clips, 2 * rows, width), bf16),
+            pltpu.VMEM((width, 3 * half), bf16),
+            pltpu.VMEM((clips, 4, 1, rows), f32),
             pltpu.VMEM((clips, rows, width), bf16),
             pltpu.VMEM((clips, 3, rows, width), bf16),
-            pltpu.VMEM((clips, 2 * pairs, rows, lanes), bf16),
             pltpu.VMEM((clips, pairs, rows, lanes), bf16),
+            pltpu.VMEM((clips, pairs, rows, lanes), bf16),
+            pltpu.VMEM((rows, half), bf16),
             pltpu.VMEM((8, width), f32),
             pltpu.SemaphoreType.DMA((clips, 3)),
             pltpu.SemaphoreType.DMA((clips, 3)),
             pltpu.SemaphoreType.DMA((clips, pairs)),
             pltpu.SemaphoreType.DMA((clips, pairs)),
+            pltpu.SemaphoreType.DMA((clips, 4)),
+            pltpu.SemaphoreType.DMA(()),
         ],
         compiler_params=params(collective_id=0, has_side_effects=True),
         cost_estimate=pl.CostEstimate(
@@ -1399,7 +1439,7 @@
             clip_size, tokens, kept_counts, attn_gain, attn_shift, qkv_weight, query_bias, value_bias,
             proj_weight, proj_bias, mlp_gain, mlp_shift, fc1_weight, fc1_bias, fc2_weight, fc2_bias, cotangent,
         )
-    q, k, v, normed, part, lse, mask, weight_half, mixed, middle, normed2 = forward(
+    q, k, v, normed, weight_half, part, lse, mask, mixed, middle, normed2 = forward(
         kept_counts, tokens, rows, qkv_weight, query_bias, value_bias, attn_gain, attn_shift,
         proj_weight, proj_bias, mlp_gain, mlp_shift,
     )

time: 246 us -> 234 us (0.951)
  Pallas kernels: 244 us -> 232 us
    pallas_call x1, Pallas kernels: 75 us -> 61.4 us  [forward(): pl.pallas_call(functools.partial(forward_kernel, (clips, slots, rows, pai...]
where the time goes in v2:
time: 234 us
  Pallas kernels  232 us (99%)
    pallas_call x1, Pallas kernels, backward(): pl.pallas_call(functools.partial(backward_kernel, (clips, slots, rows, bi...  113 us
    pallas_call x1, Pallas kernels, forward(): pl.pallas_call(functools.partial(forward_kernel, (clips, slots, rows, pai...  61.4 us
    pallas_call x1, Pallas kernels, mlp(): pl.pallas_call(functools.partial(mlp_kernel, (clips, slots, rows, tile)),...  50.9 us
    pallas_call x1, Pallas kernels, final_outputs(): pl.pallas_call(outputs_kernel, grid=(gtok.shape[0],), in_specs=[fixed(a.s...  6.1 us

profile of v2, /device:TPU:0, one launch (start us, length us, event | category | flops | bytes accessed | tf_op | source)
XLA Modules:
  0.0 233.9 jit_solution(7562777797487610037)
XLA Ops:
  0.6 1.3 copy.32.kept_ref
  2.0 61.4 %forward.1 = (bf16[3,608,384]{2,1,0:T(8,128)(2,1)}, bf16[3,1216,384]{2,1,0:T(8,128)(2,1)}, bf16[3,1216,384]{2,1,0:T(8,128)(2,1)}, bf16[3,608,768]{2,1,0:T(8,128)...) custom-call(s32[3,1]{1,0:T(4,128)} %copy.32.kept_ref, ...), custom_call_target="tpu_custom_call" | custom-call | flops 9861857280 | bytes 40000000 | tf_op jit(solution)/shard_map/forward/pallas_call | solution.py:278
  63.4 50.9 %mlp.1 = (bf16[3,298,768]{2,1,0:T(8,128)(2,1)}, bf16[2,768,1536]{2,1,0:T(8,128)(2,1)}, bf16[2,3072,384]{2,1,0:T(8,128)(2,1)}, bf16[2,768,384]{2,1,0:T(8,128)(2,1...) custom-call(s32[3,1]{1,0:T(4,128)} %copy.32.kept_ref, ...), custom_call_target="tpu_custom_call" | custom-call | flops 25820135424 | bytes 40000000 | tf_op jit(solution)/shard_map/mlp/pallas_call | solution.py:432
  114.3 113.4 %backward.1 = (f32[3,298,768]{2,1,0:T(8,128)}, bf16[96,3072]{1,0:T(8,128)(2,1)}, bf16[384,768]{1,0:T(8,128)(2,1)}, bf16[96,768]{1,0:T(8,128)(2,1)}, bf16[96,2304]{1,0:T(8,128)(2,1)}, /*index=5*/f32[16,768]{1,0:T(8,128)}) custom-call(bf16[3,608,384]{2,1,0:T(8,128)(2,1)} %get-tuple-element.58.q_ref, bf16[3,1216,384]{2,1,0:T(8,128)(2,1)} %get-tuple-element.59.k_ref, ...), custom_call_target="tpu_custom_call" | custom-call | flops 14972092416 | bytes 60000000 | tf_op jit(solution)/shard_map/backward/pallas_call | solution.py:927
  227.6 6.1 %final_outputs.1 = (f32[96,3072]{1,0:T(8,128)}, f32[384,768]{1,0:T(8,128)}, f32[96,768]{1,0:T(8,128)}, f32[96,2304]{1,0:T(8,128)}, f32[3,298,768]{2,1,0:T(8,128)...) custom-call(bf16[96,3072]{1,0:T(8,128)(2,1)} %get-tuple-element.73.f, ...), custom_call_target="tpu_custom_call" | custom-call | tf_op jit(solution)/shard_map/final_outputs/pallas_call | solution.py:986

commit v3 on v2

--- a/solution.py
+++ b/solution.py
@@ -78,7 +78,7 @@
 def forward_kernel(
     counts,
     kept_ref, tok_ref, qkv_ref, qb_ref, vb_ref, gain_ref, shift_ref, proj_ref, pb_ref, gain2_ref, shift2_ref,
-    q_out, k_out, v_out, normed_out, weight_out, part_ref, lse_ref, mask_ref, mixed_ref, middle_ref, normed2_ref,
+    q_out, k_out, v_out, normed_out, far_out, weight_out, part_ref, lse_ref, mask_ref, mixed_ref, middle_ref, normed2_ref,
     q_all, k_all, v_all, normed_all, weight, live_all, own, held, mix_send, mix_got, own_mix, vecs,
     tok_send, tok_recv, part_send, part_recv, out_sem, weight_sem,
 ):
@@ -135,10 +135,16 @@
             for i, (src, dst) in enumerate(
                 ((q_all, q_out), (k_all, k_out), (v_all, v_out), (normed_all, normed_out))
             )
-        ]
-
-    def weight_copy():
-        return pltpu.make_async_copy(weight, weight_out, weight_sem)
+        ] + [pltpu.make_async_copy(held.at[index, 0], far_out.at[index], out_sem.at[index, 4])]
+
+    def weight_copies():
+        moves = []
+        for pair in range(pairs):
+            for part in range(3):
+                src = weight.at[:, pl.ds(part * half + pair * lanes, lanes)]
+                dst = weight_out.at[:, pl.ds((3 * pair + part) * lanes, lanes)]
+                moves.append(pltpu.make_async_copy(src, dst, weight_sem.at[3 * pair + part]))
+        return moves
 
     @pl.when((clip == 0) & (turn == 0))
     def enter():
@@ -158,7 +164,8 @@
             vecs[i : i + 1] = row_of(ref)
         for part in range(3):
             weight[:, part * half : (part + 1) * half] = qkv_ref[:, lane_slice(part * width + vert * half, half)]
-        weight_copy().start()
+        for move in weight_copies():
+            move.start()
 
         def own_slots(index, carry):
             project(index, 0, own[index])
@@ -255,7 +262,8 @@
 
     @pl.when((turn == 1) & (clip == clips - 1))
     def leave():
-        weight_copy().wait()
+        for move in weight_copies():
+            move.wait()
         for index in range(clips):
             for move in out_copies(index):
                 move.wait()
@@ -283,7 +291,7 @@
         + [whole(proj_weight)]
         + [whole(v) for v in (proj_bias, gain2, shift2)],
         out_specs=[
-            anywhere, anywhere, anywhere, anywhere, anywhere,
+            anywhere, anywhere, anywhere, anywhere, anywhere, anywhere,
             block(2 * rows, half), block(2 * rows, half), block(1, keys),
             late, late, late,
         ],
@@ -292,6 +300,7 @@
             shape((clips, keys, half), bf16),
             shape((clips, keys, half), bf16),
             shape((clips, 2 * rows, width), bf16),
+            shape((clips, rows, width), bf16),
             shape((width, 3 * half), bf16),
             shape((clips, 2 * rows, half), bf16),
             shape((clips, 2 * rows, half), f32),
@@ -317,8 +326,8 @@
             pltpu.SemaphoreType.DMA((clips, 3)),
             pltpu.SemaphoreType.DMA((clips, pairs)),
             pltpu.SemaphoreType.DMA((clips, pairs)),
-            pltpu.SemaphoreType.DMA((clips, 4)),
-            pltpu.SemaphoreType.DMA(()),
+            pltpu.SemaphoreType.DMA((clips, 5)),
+            pltpu.SemaphoreType.DMA((3 * pairs,)),
         ],
         compiler_params=params(collective_id=0, has_side_effects=True),
         cost_estimate=pl.CostEstimate(
@@ -358,21 +367,19 @@
         out_acc[...] = jnp.zeros_like(out_acc)
         dn_acc[...] = jnp.zeros_like(dn_acc)
 
+    bias = biases[pl.ds(step, 1), :]
     hidden_ref[...] = dot(n2_ref[...], fc1_ref[...])
     dact_ref[...] = dot(grad_ref[...], fc2_ref[...], NT)
-    bias = biases[pl.ds(step, 1), :]
-
-    def gelu_tile(index, sums):
-        at = pl.ds(pl.multiple_of(index * tile, tile), tile)
-        hidden = hidden_ref[at, :] + bias
+    sums = jnp.zeros((tile, chunk), f32)
+    for begin in range(0, total, tile):
+        at = slice(begin, begin + tile)
+        hidden = hidden_ref[at] + bias
         cdf = 0.5 * (1.0 + lax.erf(hidden * (0.5 ** 0.5)))
-        active_ref[at, :] = (hidden * cdf).astype(bf16)
+        active_ref[at] = (hidden * cdf).astype(bf16)
         slope = cdf + hidden * (jnp.exp(-0.5 * hidden * hidden) * (1.0 / math.sqrt(2.0 * math.pi)))
-        dhid = (dact_ref[at, :] * slope).astype(bf16)
-        dhid_ref[at, :] = dhid
-        return sums + dhid.astype(f32)
-
-    sums = lax.fori_loop(0, total // tile, gelu_tile, jnp.zeros((tile, chunk), f32))
+        dhid = (dact_ref[at] * slope).astype(bf16)
+        dhid_ref[at] = dhid
+        sums = sums + dhid.astype(f32)
     db1_ref[...] = column_sums(sums)
     active = active_ref[...]
     dhid = dhid_ref[...]
@@ -388,15 +395,13 @@
     def finish():
         gain = row_of(gain_ref)
         bias2 = row_of(b2_ref)
-        sum_gain = jnp.zeros((1, width), f32)
-        sum_shift = jnp.zeros((1, width), f32)
-        sum_grad = jnp.zeros((1, width), f32)
-        sum_proj = jnp.zeros((1, width), f32)
-        for clip in range(clips):
-            at = slice(clip * rows, (clip + 1) * rows)
+        small_ref[...] = jnp.zeros_like(small_ref)
+
+        def finish_clip(clip, carry):
+            at = pl.ds(pl.multiple_of(clip * rows, rows), rows)
             middle = middle_ref[at]
-            layer = middle[:slots] + (out_acc[clip * rows : clip * rows + slots] + bias2)
-            out_ref[clip] = (live_rows(clip, slots) * layer).astype(bf16)
+            layer = middle + (out_acc[at] + bias2)
+            out_ref[clip] = (live_rows(clip, slots) * layer[:slots]).astype(bf16)
             unit, inverse = center_scale(middle)
             grad = dn_acc[at]
             out_grad = grad_ref[at].astype(f32)
@@ -405,17 +410,16 @@
             low = gmid.astype(bf16)
             dhid_ref[at, :width] = low
             gmixed_ref[at] = dot(low, proj_ref[...], NT).astype(bf16)
-            sum_gain += column_sums(grad * unit)
-            sum_shift += column_sums(grad)
-            sum_grad += column_sums(out_grad)
-            sum_proj += column_sums(low.astype(f32))
+            small_ref[0:1] += column_sums(grad * unit)
+            small_ref[1:2] += column_sums(grad)
+            small_ref[2:3] += column_sums(out_grad)
+            small_ref[3:4] += column_sums(low.astype(f32))
+            return carry
+
+        lax.fori_loop(0, clips, finish_clip, 0)
         dproj = dot(mixed_ref[...], dhid_ref[:, :width], TN).astype(bf16)
         dproj_ref[0] = dproj[:, :half]
         dproj_ref[1] = dproj[:, half:]
-        small_ref[0:1] = sum_gain
-        small_ref[1:2] = sum_shift
-        small_ref[2:3] = sum_grad
-        small_ref[3:4] = sum_proj
 
 
 def mlp(kept, n2, middle, cot, mixed, fc1, b1, fc2, b2, gain, proj, rows):
@@ -483,55 +487,55 @@
     rows = width // clip_size
     tall = hidden // clip_size
     first, second = (0, 1, 2), (1, 0, 2)
-    cut = 5 * width // 6
+    chunks = [("qkv", i, rows // 2, width // 2, order) for i, order in enumerate(QKV_ORDERS)]
     return [
         ("fc1", 0, rows, hidden // 4, first),
         ("fc2", 0, tall // 2, width // 2, second),
         ("fc1", hidden // 4, rows, hidden // 4, first),
         ("fc2", tall // 2, tall // 2, width // 2, second),
         ("proj", 0, rows, width // 2, PROJ_ORDER),
-        ("qkv", 0, rows // 2, cut, QKV_ORDERS[0]),
-        ("qkv", cut, rows // 2, 3 * width // 2 - cut, QKV_ORDERS[1]),
-    ]
+    ] + chunks
 
 
 PROJ_ORDER = (1, 0, 2)
-QKV_ORDERS = ((1, 0, 2), (0, 1, 2))
+QKV_ORDERS = ((1, 0, 2), (1, 0, 2), (1, 0, 2))
 SUM_STEPS = {
-    3: [("end", 4, 0), ("start", 4, 1)],
-    4: [("end", 0, 0), ("start", 0, 1), ("end", 1, 0), ("end", 2, 0), ("end", 3, 0)],
-    5: [("start", 1, 1)],
-    6: [("end", 4, 1)],
-    8: [("start", 2, 1)],
-    9: [("end", 0, 1), ("start", 0, 2)],
-    10: [("end", 1, 1)],
-    11: [("start", 3, 1)],
-    12: [("end", 0, 2), ("start", 0, 3), ("start", 1, 2)],
-    13: [("end", 2, 1)],
-    14: [("start", 4, 2)],
-    15: [("end", 1, 2), ("start", 1, 3)],
-    16: [("end", 0, 3), ("start", 0, 4), ("start", 2, 2), ("end", 4, 2)],
-    17: [("start", 4, 3)],
-    18: [("end", 3, 1), ("start", 3, 2)],
-    19: [("end", 0, 4), ("start", 0, 5), ("end", 1, 3), ("start", 1, 4), ("end", 4, 3),
-        ("start", 4, 4)],
-    20: [("end", 0, 5), ("end", 2, 2), ("start", 2, 3)],
-    21: [("end", 1, 4), ("start", 1, 5), ("end", 3, 2), ("start", 3, 3), ("end", 4, 4),
-        ("start", 4, 5)],
-    22: [("end", 1, 5), ("end", 4, 5)],
-    23: [("end", 6, 0), ("start", 6, 1), ("end", 5, 0), ("start", 5, 1), ("end", 2, 3),
-        ("start", 2, 4), ("end", 3, 3), ("start", 3, 4), ("input", 2, 0), ("end", 6, 1),
-        ("start", 6, 2), ("end", 2, 4), ("start", 2, 5), ("vec", 0, 0), ("end", 5, 1),
-        ("start", 5, 2), ("end", 2, 5), ("end", 3, 4), ("start", 3, 5), ("end", 6, 2),
-        ("start", 6, 3), ("vec", 1, 0), ("end", 3, 5), ("end", 5, 2), ("start", 5, 3), ("vec", 2, 0),
-        ("end", 6, 3), ("start", 6, 4), ("end", 5, 3), ("start", 5, 4), ("vec", 3, 0), ("end", 6, 4),
-        ("start", 6, 5), ("end", 6, 5), ("end", 5, 4), ("start", 5, 5), ("vec", 4, 0), ("end", 5, 5)],
+    2: [("end", 0, 0), ("start", 0, 1), ("end", 1, 0), ("start", 1, 1)],
+    3: [("end", 2, 0)],
+    4: [("end", 3, 0), ("end", 4, 0)],
+    5: [("start", 2, 1), ("start", 3, 1)],
+    7: [("end", 0, 1), ("end", 1, 1)],
+    9: [("start", 0, 2), ("start", 1, 2)],
+    10: [("start", 4, 1)],
+    11: [("end", 2, 1), ("end", 3, 1), ("start", 3, 2)],
+    12: [("start", 2, 2)],
+    13: [("end", 0, 2), ("start", 0, 3), ("end", 1, 2)],
+    15: [("end", 3, 2), ("start", 1, 3), ("end", 4, 1), ("start", 4, 2)],
+    16: [("end", 2, 2), ("start", 2, 3)],
+    17: [("end", 0, 3), ("start", 0, 4), ("end", 4, 2)],
+    18: [("start", 3, 3)],
+    19: [("end", 5, 0), ("start", 5, 1), ("end", 1, 3), ("start", 1, 4)],
+    20: [("end", 0, 4), ("start", 0, 5), ("start", 4, 3)],
+    21: [("end", 0, 5), ("end", 2, 3), ("start", 2, 4)],
+    22: [("end", 6, 0), ("start", 6, 1), ("end", 1, 4), ("start", 1, 5)],
+    23: [("end", 5, 1), ("start", 5, 2), ("end", 6, 1), ("start", 6, 2), ("end", 7, 0),
+        ("start", 7, 1), ("end", 1, 5), ("end", 2, 4), ("start", 2, 5), ("end", 3, 3),
+        ("start", 3, 4), ("end", 4, 3), ("start", 4, 4)],
+    24: [("end", 2, 5)],
+    25: [("end", 5, 2), ("start", 5, 3), ("vec", 0, 0), ("end", 6, 2), ("start", 6, 3), ("end", 7, 1),
+        ("start", 7, 2), ("vec", 1, 0), ("input", 2, 0), ("end", 7, 2), ("start", 7, 3),
+        ("end", 6, 3), ("start", 6, 4), ("end", 5, 3), ("start", 5, 4), ("end", 3, 4),
+        ("start", 3, 5), ("vec", 2, 0), ("end", 4, 4), ("start", 4, 5), ("end", 3, 5), ("end", 6, 4),
+        ("start", 6, 5), ("end", 4, 5), ("end", 5, 4), ("start", 5, 5), ("end", 7, 3),
+        ("start", 7, 4), ("end", 6, 5), ("end", 5, 5), ("vec", 3, 0), ("end", 7, 4), ("start", 7, 5),
+        ("end", 7, 5), ("vec", 4, 0)],
 }
 
 
 def backward_kernel(
     meta,
-    q_ref, k_ref, v_ref, mask_ref, part_ref, lse_ref, normed_ref, weight_ref, tok_ref, gmid_ref, gain_ref,
+    q_ref, k_ref, v_ref, mask_ref, part_ref, lse_ref, normed_ref, weight_ref, near_ref, far_ref,
+    tok_ref, gmid_ref, gain_ref,
     small_ref, db1_ref, gmixed_ref, dfc1_ref, dfc2_ref, dproj_ref,
     gtok_ref, fc1_out, fc2_out, proj_out, qkv_out, vec_out,
     *scratch,
@@ -549,7 +553,7 @@
     take = lambda n: [scratch.pop(0) for _ in range(n)]
     (grad_all, packed, kv_acc, kv_send, kv_got, acc, dn_send, dn_got, dw_acc, bias_acc, vec_sum, vec_got) = take(12)
     own_bufs = dict(zip(("fc1", "fc2", "proj"), take(3)))
-    dw_low = {5: scratch.pop(0), 6: scratch.pop(0)}
+    dw_low = scratch.pop(0)
     stage_bufs = [take(bits + 1) for _ in arrays]
     vert_bufs = take(5)
     full_bufs = take(count)
@@ -591,7 +595,7 @@
             return dfc2_ref.at[(who,) + every + (pl.ds(at, r), slice(None))]
         if name == "proj":
             return dproj_ref.at[who]
-        return dw_low[a].at[who]
+        return dw_low.at[at, who]
 
     def chosen(a, stage, index_of):
         order = arrays[a][4]
@@ -633,7 +637,7 @@
         stage_copy(a, stage).wait_recv()
         if stage == 0:
             if name == "qkv":
-                add_blocks(stage_bufs[a][0], dw_low[a].at[core], bits)
+                add_blocks(stage_bufs[a][0], dw_low.at[arrays[a][1], core], bits)
             else:
                 own_copy(a).wait()
                 add_blocks(stage_bufs[a][0], own_bufs[name], bits)
@@ -647,7 +651,7 @@
             full_bufs[a][core] = stage_bufs[a][bits][...] + vert_bufs[a][...]
 
     def vec_copy(hop):
-        device = core_dev if hop == 0 else vert_dev if hop == 1 else clip_dev[hop - 2]
+        device = ([core_dev] + clip_dev + [vert_dev])[hop]
         return remote(vec_sum.at[hop], vec_got.at[hop], vec_out_sem.at[hop], vec_in_sem.at[hop], device)
 
     def vec_end(hop):
@@ -680,6 +684,8 @@
         for a in (0, 1, 4):
             own_copy(a).start()
         vec_sum[0] = jnp.zeros_like(vec_sum[0])
+        bias_acc[...] = jnp.zeros_like(bias_acc)
+        dw_acc[...] = jnp.zeros_like(dw_acc)
         vec_sum[0, 4:8] = small_ref[0:4]
         for i in range(db1_ref.shape[1] // width):
             vec_sum[0, 8 + i : 9 + i] = db1_ref[0:1, i * width : (i + 1) * width]
@@ -692,10 +698,7 @@
                     perform(action)
 
     def attend():
-        index = attention_index(step, places)
-        clip = index // (2 * pairs)
-        slot = (index // pairs) % 2
-        pair = index % pairs
+        clip, slot, pair = attention_unit(step, places, clips, pairs)
 
         @pl.when((pair == 0) & (slot == 0))
         def own_grads():
@@ -727,7 +730,7 @@
         first = own_lanes(dqs[0].shape, 0)
         dq = (jnp.where(first, dqs[0], dqs[1]) * DH ** -0.5).astype(bf16)
         at = pl.ds(pl.multiple_of(slot * rows, rows), rows)
-        packed[clip, at, lane_slice(pair * lanes, lanes)] = dq
+        packed[clip, at, lane_slice(3 * pair * lanes, lanes)] = dq
 
         @pl.when(slot == 0)
         def keep():
@@ -742,52 +745,93 @@
 
             for part, value in enumerate((dk, dv)):
                 low = (kv_acc[pair, part] + value).astype(bf16)
-                packed[clip, :, lane_slice((part + 1) * half + pair * lanes, lanes)] = low[: 2 * rows]
+                packed[clip, :, lane_slice((3 * pair + part + 1) * lanes, lanes)] = low[: 2 * rows]
                 kv_send[pair, part] = low[2 * rows :]
             kv_copy(clip, pair).start()
 
     is_attention = step < places["projections"][-1]
-    for at in places["projections"][:-1]:
+    for at in places["pauses"]:
         is_attention = is_attention & (step != at)
     pl.when(is_attention)(attend)
 
-    for clip in range(clips):
-        @pl.when(step == places["projections"][clip])
-        def projections(clip=clip):
-            for pair in range(pairs):
-                kv_copy(clip, pair).wait_recv()
-                for part in range(2):
-                    at = slice((part + 1) * half + pair * lanes, (part + 1) * half + (pair + 1) * lanes)
-                    packed[clip, :, at] = packed[clip, :, at] + kv_got[clip, pair, part]
-            grads = packed[clip]
-            back = dot(grads, weight_ref[...], NT)
-            acc[clip] = back[:rows]
-            dn_send[clip] = back[rows:].astype(bf16)
-            dn_copy(clip).start()
-            more = dot(normed_ref[0], grads, TN)
-            sum_q = column_sums(grads[:, :half].astype(f32))
-            sum_v = column_sums(grads[:, 2 * half :].astype(f32))
-            if clip == 0:
-                dw_acc[...] = more
-                bias_acc[0:1] = sum_q
-                bias_acc[1:2] = sum_v
-            elif clip < clips - 1:
-                dw_acc[...] += more
-                bias_acc[0:1] += sum_q
-                bias_acc[1:2] += sum_v
-            else:
-                low = (dw_acc[...] + more).astype(bf16)
-                for a, buf in dw_low.items():
-                    _, at, r, width_a, _ = arrays[a]
-                    for block in range(2 ** bits):
-                        index = tuple((block >> b) & 1 for b in range(bits)[::-1])
-                        for who in range(2):
-                            start = (2 * block + who) * r
-                            buf[(who,) + index] = low[start : start + r, at : at + width_a]
-                    stage_copy(a, 0).start()
-                mine = lane_slice(vert * half, half)
-                vec_sum[0, 2:3, mine] = bias_acc[0:1] + sum_q
-                vec_sum[0, 3:4, mine] = bias_acc[1:2] + sum_v
+    def take_pair(clip, pair):
+        kv_copy(clip, pair).wait_recv()
+        for part in range(2):
+            at = lane_slice((3 * pair + part + 1) * lanes, lanes)
+            packed[clip, :, at] = packed[clip, :, at] + kv_got[clip, pair, part]
+        at = lane_slice(pair * lanes, lanes)
+        for row, part in ((0, 0), (1, 2)):
+            value = packed[clip, :, lane_slice((3 * pair + part) * lanes, lanes)]
+            bias_acc[row : row + 1, at] += column_sums(value.astype(f32))
+
+    def norm_sums(clip, back):
+        near, _ = center_scale(near_ref[0].astype(f32))
+        far, _ = center_scale(far_ref[0].astype(f32))
+        vec_sum[0, 0:1] += column_sums(back[:slots] * near) + column_sums(back[rows:] * far)
+        vec_sum[0, 1:2] += column_sums(back)
+
+    def give_back(clip, back):
+        acc[clip] = back[:rows]
+        dn_send[clip] = back[rows:].astype(bf16)
+        dn_copy(clip).start()
+
+    def last_chunk(pair):
+        at = lane_slice(3 * pair * lanes, 3 * lanes)
+        more = dot(normed_ref[0], packed[clips - 1, :, at], TN)
+        low = (dw_acc[:, at] + more).astype(bf16)
+        r = arrays[5][2]
+        for block in range(2 ** bits):
+            index = tuple((block >> b) & 1 for b in range(bits)[::-1])
+            for who in range(2):
+                start = (2 * block + who) * r
+                dw_low[(pair, who) + index] = low[start : start + r]
+
+    early_steps = places["projections"][:-1]
+    early = functools.reduce(jnp.logical_or, [step == at for at in early_steps])
+
+    @pl.when(early)
+    def projections():
+        clip = sum((step > at).astype(jnp.int32) for at in early_steps)
+
+        def take_one(pair, carry):
+            take_pair(clip, pair)
+            return carry
+
+        lax.fori_loop(0, pairs, take_one, 0)
+        grads = packed[clip]
+        back = dot(grads, weight_ref[...], NT)
+        give_back(clip, back)
+        dw_acc[...] += dot(normed_ref[0], grads, TN)
+        norm_sums(clip, back)
+
+    chunk_steps = places["chunks"]
+
+    @pl.when(functools.reduce(jnp.logical_or, [step == at for at in chunk_steps]))
+    def chunk():
+        pair = sum((step > at).astype(jnp.int32) for at in chunk_steps)
+        take_pair(clips - 1, pair)
+        last_chunk(pair)
+
+    for pair in range(pairs - 1):
+        @pl.when(step == chunk_steps[pair])
+        def send_chunk(pair=pair):
+            stage_copy(5 + pair, 0).start()
+
+    @pl.when(step == places["projections"][-1])
+    def last_projections():
+        clip = clips - 1
+        before = 3 * (pairs - 1) * lanes
+        back = dot(packed[clip, :, :before], weight_ref[:, :before], NT)
+        take_pair(clip, pairs - 1)
+        last_chunk(pairs - 1)
+        stage_copy(4 + pairs, 0).start()
+        back = back + dot(packed[clip, :, before:], weight_ref[:, before:], NT)
+        give_back(clip, back)
+        norm_sums(clip, back)
+        mine = lane_slice(vert * half, half)
+        vec_sum[0, 2:3, mine] = bias_acc[0:1]
+        vec_sum[0, 3:4, mine] = bias_acc[1:2]
+        vec_copy(0).start()
 
     def inputs(clip):
         dn_copy(clip).wait_recv()
@@ -795,13 +839,10 @@
         unit, inverse = center_scale(tok_ref[0].astype(f32))
         result = gmid_ref[0][:slots] + norm_back(unit, inverse, row_of(gain_ref), grad[:slots])
         gtok_ref[0] = result
-        vec_sum[0, 0:1] += column_sums(grad[:slots] * unit)
-        vec_sum[0, 1:2] += column_sums(grad[:slots])
-        if clip == clips - 1:
-            vec_copy(0).start()
-
-    for clip in range(clips - 1):
-        pl.when(step == places["inputs"] + clip)(functools.partial(inputs, clip))
+
+    @pl.when((step >= places["inputs"]) & (step < places["end"]))
+    def early_inputs():
+        inputs(step - places["inputs"])
 
     @pl.when(step == places["end"])
     def finish():
@@ -822,10 +863,10 @@
                     proj_out[:, who * width_a : (who + 1) * width_a] = full[who]
                 else:
                     for side in range(2):
-                        for start in range(0, width_a, lanes):
-                            part, inside = divmod(at + start, half)
-                            to = part * width + side * half + inside
-                            qkv_out[who * r : (who + 1) * r, to : to + lanes] = full[who, side, :, start : start + lanes]
+                        for part in range(3):
+                            to = part * width + side * half + at * lanes
+                            value = full[who, side, :, part * lanes : (part + 1) * lanes]
+                            qkv_out[who * r : (who + 1) * r, to : to + lanes] = value
         vec_out[...] = vec_sum[bits + 2]
         for a in range(count):
             for stage in range(bits + 3):
@@ -841,19 +882,27 @@
 
 def step_places(clips, pairs):
     of_clip = 2 * pairs
-    projections = [of_clip * (c + 1) + 2 + c for c in range(clips - 1)] + [of_clip * clips + clips - 1]
+    projections = [of_clip * (c + 1) + 2 + c for c in range(clips - 1)]
+    begin = of_clip * (clips - 1) + clips - 1
+    chunks = [begin + 2 * (pair + 1) + 1 + pair for pair in range(pairs - 1)]
+    projections.append(begin + of_clip + pairs - 1)
     inputs = projections[-1] + 1
-    return {"projections": projections, "inputs": inputs, "end": inputs + clips - 1}
-
-
-def attention_index(step, places):
+    pauses = projections[:-1] + chunks
+    return {"projections": projections, "chunks": chunks, "pauses": pauses, "inputs": inputs, "end": inputs + clips - 1}
+
+
+def attention_unit(step, places, clips, pairs):
     index = step
-    for at in places["projections"][:-1]:
+    for at in places["pauses"]:
         index = index - (step > at).astype(jnp.int32)
-    return index
-
-
-def backward(q, k, v, mask, part, lse, normed, weight_half, tokens, gmid, gain, small, db1, gmixed,
+    index = jnp.minimum(index, 2 * clips * pairs - 1)
+    clip = index // (2 * pairs)
+    inside = index % (2 * pairs)
+    last = clip == clips - 1
+    return clip, jnp.where(last, inside % 2, inside // pairs), jnp.where(last, inside // 2, inside % pairs)
+
+
+def backward(q, k, v, mask, part, lse, normed, weight_half, tokens, far, gmid, gain, small, db1, gmixed,
              dfc1, dfc2, dproj, clip_size):
     clips, slots, width = tokens.shape
     rows = gmid.shape[1]
@@ -868,8 +917,7 @@
     one = pl.Buffered(buffer_count=1)
 
     def of_pair(s):
-        at = jnp.minimum(attention_index(s, places), 2 * clips * pairs - 1)
-        return at // (2 * pairs), (at // pairs) % 2, at % pairs
+        return attention_unit(s, places, clips, pairs)
 
     def of_keys(s):
         clip, _, pair = of_pair(s)
@@ -912,7 +960,7 @@
         vmem(*blocks, r_fc2 // 2, half),
         vmem(*blocks, r_fc1, half),
     ]
-    scratch += [vmem(2, *blocks, r, w) for name, _, r, w, _ in arrays if name == "qkv"]
+    scratch.append(vmem(pairs, 2, *blocks, r_fc1 // 2, half))
     for _, _, r, w, _ in arrays:
         scratch += [vmem(*((2,) * (bits - stage)), r, w) for stage in range(bits + 1)]
     scratch += [vmem(r, w) for name, _, r, w, _ in arrays if name != "qkv"]
@@ -933,6 +981,8 @@
             tok_pair, tok_pair,
             pl.BlockSpec((1, 2 * rows, width), of_projection),
             fixed(weight_half.shape),
+            pl.BlockSpec((1, slots, width), of_projection),
+            pl.BlockSpec((1, rows, width), of_projection),
             pl.BlockSpec((1, slots, width), of_clip),
             pl.BlockSpec((1, rows, width), of_clip),
             fixed((width,)), fixed((8, width)), fixed((1, hidden)),
@@ -959,7 +1009,7 @@
             transcendentals=clips * rows * keys * HEADS,
         ),
         name="backward",
-    )(q, k, v, mask, part, lse, normed, weight_half, tokens, gmid, gain, small, db1, gmixed, dfc1, dfc2, dproj)
+    )(q, k, v, mask, part, lse, normed, weight_half, tokens, far, tokens, gmid, gain, small, db1, gmixed, dfc1, dfc2, dproj)
 
 
 def outputs_kernel(fc1, fc2, proj, qkv, vec, gtok, fc1_out, fc2_out, proj_out, qkv_out, gtok_out, db1_out, *outs):
@@ -1439,7 +1489,7 @@
             clip_size, tokens, kept_counts, attn_gain, attn_shift, qkv_weight, query_bias, value_bias,
             proj_weight, proj_bias, mlp_gain, mlp_shift, fc1_weight, fc1_bias, fc2_weight, fc2_bias, cotangent,
         )
-    q, k, v, normed, weight_half, part, lse, mask, mixed, middle, normed2 = forward(
+    q, k, v, normed, far, weight_half, part, lse, mask, mixed, middle, normed2 = forward(
         kept_counts, tokens, rows, qkv_weight, query_bias, value_bias, attn_gain, attn_shift,
         proj_weight, proj_bias, mlp_gain, mlp_shift,
     )
@@ -1450,7 +1500,7 @@
     )
     by_clip = lambda a: a.reshape(clips, rows, width)
     gtok, low_fc1, low_fc2, low_proj, low_qkv, summed = backward(
-        q, k, v, mask, part, lse, normed, weight_half, tokens, by_clip(gmid), attn_gain, small, db1,
+        q, k, v, mask, part, lse, normed, weight_half, tokens, far, by_clip(gmid), attn_gain, small, db1,
         by_clip(gmixed), dfc1, dfc2, dproj, clip_size,
     )
     fc1, fc2, proj, qkv, grad_tokens, fc1_b, *rows_out = final_outputs(

time: 234 us -> 226 us (0.966)
  Pallas kernels: 232 us -> 224 us
    pallas_call x1, Pallas kernels: 50.9 us -> 42.6 us  [mlp(): pl.pallas_call(functools.partial(mlp_kernel, (clips, slots, rows, tile)),...]
where the time goes in v3:
time: 226 us
  Pallas kernels  224 us (99%)
    pallas_call x1, Pallas kernels, backward(): pl.pallas_call(functools.partial(backward_kernel, (clips, slots, rows, bi...  114 us
    pallas_call x1, Pallas kernels, forward(): pl.pallas_call(functools.partial(forward_kernel, (clips, slots, rows, pai...  61.5 us
    pallas_call x1, Pallas kernels, mlp(): pl.pallas_call(functools.partial(mlp_kernel, (clips, slots, rows, tile)),...  42.6 us
    pallas_call x1, Pallas kernels, final_outputs(): pl.pallas_call(outputs_kernel, grid=(gtok.shape[0],), in_specs=[fixed(a.s...  6.1 us

profile of v3, /device:TPU:0, one launch (start us, length us, event | category | flops | bytes accessed | tf_op | source)
XLA Modules:
  0.0 226.2 jit_solution(11075624887894547259)
XLA Ops:
  0.6 1.3 copy.32.kept_ref
  2.0 61.5 %forward.1 = (bf16[3,608,384]{2,1,0:T(8,128)(2,1)}, bf16[3,1216,384]{2,1,0:T(8,128)(2,1)}, bf16[3,1216,384]{2,1,0:T(8,128)(2,1)}, bf16[3,608,768]{2,1,0:T(8,128)...) custom-call(s32[3,1]{1,0:T(4,128)} %copy.32.kept_ref, ...), custom_call_target="tpu_custom_call" | custom-call | flops 9861857280 | bytes 40000000 | tf_op jit(solution)/shard_map/forward/pallas_call | solution.py:286
  63.4 42.6 %mlp.1 = (bf16[3,298,768]{2,1,0:T(8,128)(2,1)}, bf16[2,768,1536]{2,1,0:T(8,128)(2,1)}, bf16[2,3072,384]{2,1,0:T(8,128)(2,1)}, bf16[2,768,384]{2,1,0:T(8,128)(2,1...) custom-call(s32[3,1]{1,0:T(4,128)} %copy.32.kept_ref, ...), custom_call_target="tpu_custom_call" | custom-call | flops 25820135424 | bytes 40000000 | tf_op jit(solution)/shard_map/mlp/pallas_call | solution.py:436
  106.0 113.9 %backward.1 = (f32[3,298,768]{2,1,0:T(8,128)}, bf16[96,3072]{1,0:T(8,128)(2,1)}, bf16[384,768]{1,0:T(8,128)(2,1)}, bf16[96,768]{1,0:T(8,128)(2,1)}, bf16[96,2304]{1,0:T(8,128)(2,1)}, /*index=5*/f32[16,768]{1,0:T(8,128)}) custom-call(bf16[3,608,384]{2,1,0:T(8,128)(2,1)} %get-tuple-element.59.q_ref, bf16[3,1216,384]{2,1,0:T(8,128)(2,1)} %get-tuple-element.60.k_ref, ...), custom_call_target="tpu_custom_call" | custom-call | flops 14972092416 | bytes 60000000 | tf_op jit(solution)/shard_map/backward/pallas_call | solution.py:975
  220.0 6.1 %final_outputs.1 = (f32[96,3072]{1,0:T(8,128)}, f32[384,768]{1,0:T(8,128)}, f32[96,768]{1,0:T(8,128)}, f32[96,2304]{1,0:T(8,128)}, f32[3,298,768]{2,1,0:T(8,128)...) custom-call(bf16[96,3072]{1,0:T(8,128)(2,1)} %get-tuple-element.75.f, ...), custom_call_target="tpu_custom_call" | custom-call | tf_op jit(solution)/shard_map/final_outputs/pallas_call | solution.py:1036

commit v4 on v3

--- a/solution.py
+++ b/solution.py
@@ -153,7 +153,7 @@
             pl.semaphore_signal(barrier, inc=1, device_id=device, device_id_type=mesh_id)
         first = (slots // 16) * 16
         for index in range(clips):
-            kept = (kept_ref[index, 0] - slots // 2).astype(f32).astype(bf16)
+            kept = (kept_ref[index] - slots // 2).astype(f32).astype(bf16)
             own[index, first:] = jnp.broadcast_to(kept, (rows - first, width))
             own[index, :slots] = tok_ref[index]
         pl.semaphore_wait(barrier, 2)
@@ -218,18 +218,20 @@
 
     at = pl.ds(pl.multiple_of(slot * rows, rows), rows)
     live = mask_ref[0] > 0.5
+    ones = jnp.ones((4 * rows, lanes), bf16)
     for pair in range(pairs):
         here = slice(pair * lanes, (pair + 1) * lanes)
         keys = k_all[clip, :, here]
-        values = v_all[clip, :, here]
+        values = jnp.concatenate([v_all[clip, :, here], ones], axis=1)
         query = q_all[clip, at, here]
         outs, lses = [], []
         for head in range(2):
             scores = jnp.where(live, dot(only(query, head), keys, NT), MASKED)
             top = jnp.max(scores, axis=1, keepdims=True)
             exps = jnp.exp(scores - top)
-            total = jnp.sum(exps, axis=1, keepdims=True)
-            outs.append(dot(exps.astype(bf16), values) / total)
+            both = dot(exps.astype(bf16), values)
+            total = both[:, lanes:]
+            outs.append(both[:, :lanes] / total)
             lses.append(top + jnp.log(total))
         first = own_lanes(outs[0].shape, 0)
         mixed = jnp.where(first, outs[0], outs[1]).astype(bf16)
@@ -339,8 +341,9 @@
 
 def mlp_kernel(
     counts,
-    kept_ref, n2_ref, middle_ref, cot_ref, mixed_ref, fc1_ref, b1_ref, fc2_ref, b2_ref, gain_ref, proj_ref,
-    out_ref, dfc1_ref, dfc2_ref, dproj_ref, db1_ref, small_ref, gmid_ref, gmixed_ref,
+    kept_ref, n2_ref, middle_hbm, cot_ref, mixed_hbm, fc1_ref, b1_ref, fc2_ref, b2_ref, gain_ref, proj_hbm,
+    out_ref, dfc1_ref, dfc2_ref, dproj_ref, db1_ref, small_ref, gmid_hbm, gmixed_hbm,
+    middle_ref, mixed_ref, proj_ref, gmixed_ref, in_sems, out_sems,
     n2t_ref, grad_ref, out_acc, dn_acc, hidden_ref, dact_ref, active_ref, dhid_ref, biases,
 ):
     clips, slots, rows, tile = counts
@@ -351,10 +354,23 @@
 
     def live_rows(clip, size):
         slot = lax.broadcasted_iota(jnp.int32, (size, 1), 0)
-        return (slot < kept_ref[clip, 0]).astype(f32)
+        return (slot < kept_ref[clip]).astype(f32)
+
+    def loads():
+        pairs = ((middle_hbm, middle_ref), (mixed_hbm, mixed_ref), (proj_hbm, proj_ref))
+        return [pltpu.make_async_copy(src, dst, in_sems.at[i]) for i, (src, dst) in enumerate(pairs)]
+
+    def stores(clip):
+        at = pl.ds(pl.multiple_of(clip * rows, rows), rows)
+        pairs = ((middle_ref, gmid_hbm), (gmixed_ref, gmixed_hbm))
+        return [
+            pltpu.make_async_copy(src.at[at], dst.at[at], out_sems.at[clip, i]) for i, (src, dst) in enumerate(pairs)
+        ]
 
     @pl.when(step == 0)
     def start():
+        for load in loads():
+            load.start()
         n2t_ref[...] = n2_ref[...].T
         first = (slots // 16) * 16
         for clip in range(clips):
@@ -393,6 +409,8 @@
 
     @pl.when(step == pl.num_programs(0) - 1)
     def finish():
+        for load in loads():
+            load.wait()
         gain = row_of(gain_ref)
         bias2 = row_of(b2_ref)
         small_ref[...] = jnp.zeros_like(small_ref)
@@ -406,7 +424,7 @@
             grad = dn_acc[at]
             out_grad = grad_ref[at].astype(f32)
             gmid = out_grad + norm_back(unit, inverse, gain, grad)
-            gmid_ref[at] = gmid
+            middle_ref[at] = gmid
             low = gmid.astype(bf16)
             dhid_ref[at, :width] = low
             gmixed_ref[at] = dot(low, proj_ref[...], NT).astype(bf16)
@@ -414,12 +432,17 @@
             small_ref[1:2] += column_sums(grad)
             small_ref[2:3] += column_sums(out_grad)
             small_ref[3:4] += column_sums(low.astype(f32))
+            for store in stores(clip):
+                store.start()
             return carry
 
         lax.fori_loop(0, clips, finish_clip, 0)
         dproj = dot(mixed_ref[...], dhid_ref[:, :width], TN).astype(bf16)
         dproj_ref[0] = dproj[:, :half]
         dproj_ref[1] = dproj[:, half:]
+        for clip in range(clips):
+            for store in stores(clip):
+                store.wait()
 
 
 def mlp(kept, n2, middle, cot, mixed, fc1, b1, fc2, b2, gain, proj, rows):
@@ -431,6 +454,7 @@
     half = steps // 2
     tile = 16
     whole = lambda a: pl.BlockSpec(a.shape, lambda j: (0,) * a.ndim, pipeline_mode=one)
+    anywhere = pl.BlockSpec(memory_space=pl.ANY)
     one = pl.Buffered(buffer_count=1)
     big = pl.BlockSpec((total, width), lambda j: (0, 0), pipeline_mode=one)
     return pl.pallas_call(
@@ -438,11 +462,11 @@
         grid=(steps,),
         in_specs=[
             pl.BlockSpec(memory_space=pltpu.SMEM),
-            big, big, whole(cot), big,
+            big, anywhere, whole(cot), anywhere,
             pl.BlockSpec((width, chunk), lambda j: (0, j)),
             whole(b1),
             pl.BlockSpec((chunk, width), lambda j: (j, 0)),
-            whole(b2), whole(gain), whole(proj),
+            whole(b2), whole(gain), anywhere,
         ],
         out_specs=[
             full((clips, slots, width)),
@@ -451,8 +475,8 @@
             full((2, width, width // 2)),
             pl.BlockSpec((1, chunk), lambda j: (0, j)),
             full((8, width)),
-            full((total, width)),
-            full((total, width)),
+            anywhere,
+            anywhere,
         ],
         out_shape=[
             jax.ShapeDtypeStruct((clips, slots, width), bf16),
@@ -465,6 +489,12 @@
             jax.ShapeDtypeStruct((total, width), bf16),
         ],
         scratch_shapes=[
+            pltpu.VMEM((total, width), f32),
+            pltpu.VMEM((total, width), bf16),
+            pltpu.VMEM((width, width), bf16),
+            pltpu.VMEM((total, width), bf16),
+            pltpu.SemaphoreType.DMA((3,)),
+            pltpu.SemaphoreType.DMA((clips, 2)),
             pltpu.VMEM((width, total), bf16),
             pltpu.VMEM((total, width), bf16),
             pltpu.VMEM((total, width), f32),
@@ -1014,11 +1044,11 @@
 
 def outputs_kernel(fc1, fc2, proj, qkv, vec, gtok, fc1_out, fc2_out, proj_out, qkv_out, gtok_out, db1_out, *outs):
     gtok_out[...] = gtok[...]
+    for src, dst in ((fc1, fc1_out), (fc2, fc2_out), (proj, proj_out), (qkv, qkv_out)):
+        dst[...] = src[...].astype(f32)
 
     @pl.when(pl.program_id(0) == 0)
     def others():
-        for src, dst in ((fc1, fc1_out), (fc2, fc2_out), (proj, proj_out), (qkv, qkv_out)):
-            dst[...] = src[...].astype(f32)
         width = vec.shape[1]
         for i, dst in enumerate(outs):
             dst[...] = vec[i : i + 1].reshape(width)
@@ -1028,16 +1058,23 @@
 
 def final_outputs(low_fc1, low_fc2, low_proj, low_qkv, summed, gtok, hidden):
     width = summed.shape[1]
+    steps = gtok.shape[0]
     one = pl.Buffered(buffer_count=1)
     fixed = lambda shape: pl.BlockSpec(shape, lambda c: (0,) * len(shape), pipeline_mode=one)
     by_clip = pl.BlockSpec((1,) + gtok.shape[1:], lambda c: (c, 0, 0))
     shape = jax.ShapeDtypeStruct
     lows = (low_fc1, low_fc2, low_proj, low_qkv)
+
+    def by_rows(a):
+        if a.shape[0] % (16 * steps):
+            return fixed(a.shape)
+        return pl.BlockSpec((a.shape[0] // steps, a.shape[1]), lambda c: (c, 0))
+
     return pl.pallas_call(
         outputs_kernel,
-        grid=(gtok.shape[0],),
-        in_specs=[fixed(a.shape) for a in lows] + [fixed(summed.shape), by_clip],
-        out_specs=[fixed(a.shape) for a in lows] + [by_clip, fixed((hidden,))] + [fixed((width,))] * 8,
+        grid=(steps,),
+        in_specs=[by_rows(a) for a in lows] + [fixed(summed.shape), by_clip],
+        out_specs=[by_rows(a) for a in lows] + [by_clip, fixed((hidden,))] + [fixed((width,))] * 8,
         out_shape=[shape(a.shape, f32) for a in lows]
         + [shape(gtok.shape, f32), shape((hidden,), f32)]
         + [shape((width,), f32)] * 8,
@@ -1429,7 +1466,7 @@
     )
     flat = lambda a: a.reshape(total, width)
     layer_out, dfc1, dfc2, dproj, db1, small2, gmid, gmixed = mlp(
-        kept_counts, flat(normed2), flat(middle), cotangent, flat(mixed), fc1_weight, fc1_bias,
+        kept_counts.reshape(clips), flat(normed2), flat(middle), cotangent, flat(mixed), fc1_weight, fc1_bias,
         fc2_weight, fc2_bias, mlp_gain, proj_weight, rows,
     )
     early = total_sum(jnp.concatenate([small2[:4].reshape(-1), db1.reshape(-1)])[None, :], clip_size)[0]
@@ -1489,13 +1526,14 @@
             clip_size, tokens, kept_counts, attn_gain, attn_shift, qkv_weight, query_bias, value_bias,
             proj_weight, proj_bias, mlp_gain, mlp_shift, fc1_weight, fc1_bias, fc2_weight, fc2_bias, cotangent,
         )
+    kept = kept_counts.reshape(clips)
     q, k, v, normed, far, weight_half, part, lse, mask, mixed, middle, normed2 = forward(
-        kept_counts, tokens, rows, qkv_weight, query_bias, value_bias, attn_gain, attn_shift,
+        kept, tokens, rows, qkv_weight, query_bias, value_bias, attn_gain, attn_shift,
         proj_weight, proj_bias, mlp_gain, mlp_shift,
     )
     flat = lambda a: a.reshape(clips * rows, width)
     layer_out, dfc1, dfc2, dproj, db1, small, gmid, gmixed = mlp(
-        kept_counts, flat(normed2), flat(middle), cotangent, flat(mixed), fc1_weight, fc1_bias,
+        kept, flat(normed2), flat(middle), cotangent, flat(mixed), fc1_weight, fc1_bias,
         fc2_weight, fc2_bias, mlp_gain, proj_weight, rows,
     )
     by_clip = lambda a: a.reshape(clips, rows, width)

time: 226 us -> 222 us (0.982)
  Pallas kernels: 224 us -> 221 us
    pallas_call x1, Pallas kernels: 42.6 us -> 39.8 us  [mlp(): pl.pallas_call(functools.partial(mlp_kernel, (clips, slots, rows, tile)),...]
where the time goes in v4:
time: 222 us
  Pallas kernels  221 us (100%)
    pallas_call x1, Pallas kernels, backward(): pl.pallas_call(functools.partial(backward_kernel, (clips, slots, rows, bi...  114 us
    pallas_call x1, Pallas kernels, forward(): pl.pallas_call(functools.partial(forward_kernel, (clips, slots, rows, pai...  61.2 us
    pallas_call x1, Pallas kernels, mlp(): pl.pallas_call(functools.partial(mlp_kernel, (clips, slots, rows, tile)),...  39.8 us
    pallas_call x1, Pallas kernels, final_outputs(): pl.pallas_call(outputs_kernel, grid=(steps,), in_specs=[by_rows(a) for a...  5.84 us

profile of v4, /device:TPU:0, one launch (start us, length us, event | category | flops | bytes accessed | tf_op | source)
XLA Modules:
  0.0 221.6 jit_solution(7037395074243749286)
XLA Ops:
  0.6 61.2 %forward.1 = (bf16[3,608,384]{2,1,0:T(8,128)(2,1)}, bf16[3,1216,384]{2,1,0:T(8,128)(2,1)}, bf16[3,1216,384]{2,1,0:T(8,128)(2,1)}, bf16[3,608,768]{2,1,0:T(8,128)...) custom-call(s32[3]{0:T(128)} %bitcast.9, ...), custom_call_target="tpu_custom_call" | custom-call | flops 9861857280 | bytes 40000000 | tf_op jit(solution)/shard_map/forward/pallas_call | solution.py:288
  61.8 39.8 %mlp.1 = (bf16[3,298,768]{2,1,0:T(8,128)(2,1)}, bf16[2,768,1536]{2,1,0:T(8,128)(2,1)}, bf16[2,3072,384]{2,1,0:T(8,128)(2,1)}, bf16[2,768,384]{2,1,0:T(8,128)(2,1...) custom-call(s32[3]{0:T(128)} %bitcast.10, ...), custom_call_target="tpu_custom_call" | custom-call | flops 25820135424 | bytes 40000000 | tf_op jit(solution)/shard_map/mlp/pallas_call | solution.py:460
  101.7 113.9 %backward.1 = (f32[3,298,768]{2,1,0:T(8,128)}, bf16[96,3072]{1,0:T(8,128)(2,1)}, bf16[384,768]{1,0:T(8,128)(2,1)}, bf16[96,768]{1,0:T(8,128)(2,1)}, bf16[96,2304]{1,0:T(8,128)(2,1)}, /*index=5*/f32[16,768]{1,0:T(8,128)}) custom-call(bf16[3,608,384]{2,1,0:T(8,128)(2,1)} %get-tuple-element.59.q_ref, bf16[3,1216,384]{2,1,0:T(8,128)(2,1)} %get-tuple-element.60.k_ref, ...), custom_call_target="tpu_custom_call" | custom-call | flops 14972092416 | bytes 60000000 | tf_op jit(solution)/shard_map/backward/pallas_call | solution.py:1005
  215.6 5.8 %final_outputs.1 = (f32[96,3072]{1,0:T(8,128)}, f32[384,768]{1,0:T(8,128)}, f32[96,768]{1,0:T(8,128)}, f32[96,2304]{1,0:T(8,128)}, f32[3,298,768]{2,1,0:T(8,128)...) custom-call(bf16[96,3072]{1,0:T(8,128)(2,1)} %get-tuple-element.75.f, ...), custom_call_target="tpu_custom_call" | custom-call | tf_op jit(solution)/shard_map/final_outputs/pallas_call | solution.py:1073

commit v5 on v4

--- a/solution.py
+++ b/solution.py
@@ -527,38 +527,33 @@
     ] + chunks
 
 
-PROJ_ORDER = (1, 0, 2)
-QKV_ORDERS = ((1, 0, 2), (1, 0, 2), (1, 0, 2))
+PROJ_ORDER = (0, 1, 2)
+QKV_ORDERS = ((0, 1, 2), (0, 1, 2), (1, 0, 2))
 SUM_STEPS = {
     2: [("end", 0, 0), ("start", 0, 1), ("end", 1, 0), ("start", 1, 1)],
     3: [("end", 2, 0)],
     4: [("end", 3, 0), ("end", 4, 0)],
-    5: [("start", 2, 1), ("start", 3, 1)],
+    6: [("start", 2, 1), ("start", 3, 1)],
     7: [("end", 0, 1), ("end", 1, 1)],
-    9: [("start", 0, 2), ("start", 1, 2)],
-    10: [("start", 4, 1)],
-    11: [("end", 2, 1), ("end", 3, 1), ("start", 3, 2)],
-    12: [("start", 2, 2)],
-    13: [("end", 0, 2), ("start", 0, 3), ("end", 1, 2)],
-    15: [("end", 3, 2), ("start", 1, 3), ("end", 4, 1), ("start", 4, 2)],
-    16: [("end", 2, 2), ("start", 2, 3)],
-    17: [("end", 0, 3), ("start", 0, 4), ("end", 4, 2)],
-    18: [("start", 3, 3)],
-    19: [("end", 5, 0), ("start", 5, 1), ("end", 1, 3), ("start", 1, 4)],
-    20: [("end", 0, 4), ("start", 0, 5), ("start", 4, 3)],
-    21: [("end", 0, 5), ("end", 2, 3), ("start", 2, 4)],
-    22: [("end", 6, 0), ("start", 6, 1), ("end", 1, 4), ("start", 1, 5)],
-    23: [("end", 5, 1), ("start", 5, 2), ("end", 6, 1), ("start", 6, 2), ("end", 7, 0),
-        ("start", 7, 1), ("end", 1, 5), ("end", 2, 4), ("start", 2, 5), ("end", 3, 3),
-        ("start", 3, 4), ("end", 4, 3), ("start", 4, 4)],
-    24: [("end", 2, 5)],
-    25: [("end", 5, 2), ("start", 5, 3), ("vec", 0, 0), ("end", 6, 2), ("start", 6, 3), ("end", 7, 1),
-        ("start", 7, 2), ("vec", 1, 0), ("input", 2, 0), ("end", 7, 2), ("start", 7, 3),
-        ("end", 6, 3), ("start", 6, 4), ("end", 5, 3), ("start", 5, 4), ("end", 3, 4),
-        ("start", 3, 5), ("vec", 2, 0), ("end", 4, 4), ("start", 4, 5), ("end", 3, 5), ("end", 6, 4),
-        ("start", 6, 5), ("end", 4, 5), ("end", 5, 4), ("start", 5, 5), ("end", 7, 3),
-        ("start", 7, 4), ("end", 6, 5), ("end", 5, 5), ("vec", 3, 0), ("end", 7, 4), ("start", 7, 5),
-        ("end", 7, 5), ("vec", 4, 0)],
+    9: [("end", 2, 1), ("start", 0, 2), ("start", 1, 2), ("end", 3, 1)],
+    10: [("start", 2, 2), ("start", 3, 2)],
+    11: [("end", 0, 2), ("start", 0, 3), ("end", 1, 2)],
+    12: [("end", 2, 2), ("start", 1, 3), ("start", 4, 1), ("end", 3, 2)],
+    13: [("end", 0, 3), ("start", 0, 4), ("start", 2, 3)],
+    15: [("end", 5, 0), ("start", 5, 1), ("start", 3, 3), ("end", 0, 4), ("start", 0, 5),
+        ("end", 1, 3), ("start", 1, 4), ("end", 4, 1)],
+    16: [("end", 0, 5), ("start", 4, 2), ("end", 2, 3), ("start", 2, 4)],
+    17: [("end", 5, 1), ("start", 5, 2), ("end", 6, 0), ("start", 6, 1), ("end", 7, 0),
+        ("start", 7, 1), ("end", 1, 4), ("start", 1, 5), ("end", 2, 4), ("start", 2, 5),
+        ("end", 3, 3), ("start", 3, 4), ("end", 4, 2), ("start", 4, 3)],
+    18: [("end", 1, 5), ("end", 2, 5)],
+    19: [("end", 5, 2), ("start", 5, 3), ("vec", 0, 0), ("end", 6, 1), ("start", 6, 2), ("end", 7, 1),
+        ("start", 7, 2), ("end", 4, 3), ("start", 4, 4), ("vec", 1, 0), ("input", 2, 0),
+        ("end", 6, 2), ("start", 6, 3), ("end", 5, 3), ("start", 5, 4), ("end", 7, 2),
+        ("start", 7, 3), ("end", 3, 4), ("start", 3, 5), ("vec", 2, 0), ("end", 4, 4),
+        ("start", 4, 5), ("end", 3, 5), ("end", 5, 4), ("start", 5, 5), ("end", 4, 5), ("end", 6, 3),
+        ("start", 6, 4), ("end", 5, 5), ("end", 7, 3), ("start", 7, 4), ("vec", 3, 0), ("end", 6, 4),
+        ("start", 6, 5), ("end", 7, 4), ("start", 7, 5), ("end", 6, 5), ("end", 7, 5), ("vec", 4, 0)],
 }
 
 
@@ -727,8 +722,29 @@
                 for action in SUM_STEPS[at]:
                     perform(action)
 
-    def attend():
-        clip, slot, pair = attention_unit(step, places, clips, pairs)
+    def head_back(head, query, keys, values, grad, mixed, lse, live):
+        own_query, own_grad = only(query, head), only(grad, head)
+        scores = jnp.where(live, dot(own_query, keys, NT), MASKED)
+        probs = jnp.exp(scores - lse[:, head * DH : head * DH + 1])
+        delta = jnp.sum(only(grad.astype(f32) * mixed.astype(f32), head), axis=1, keepdims=True)
+        dscores = (probs * (dot(own_grad, values, NT) - delta)).astype(bf16)
+        return probs.astype(bf16), dscores, dot(dscores, keys)
+
+    def join_heads(dqs):
+        first = own_lanes(dqs[0].shape, 0)
+        return (jnp.where(first, dqs[0], dqs[1]) * DH ** -0.5).astype(bf16)
+
+    def send_pair(clip, pair, dk, dv):
+        for part, value in enumerate((dk, dv)):
+            low = value.astype(bf16)
+            packed[clip, :, lane_slice((3 * pair + part + 1) * lanes, lanes)] = low[: 2 * rows]
+            kv_send[pair, part] = low[2 * rows :]
+        kv_copy(clip, pair).start()
+
+    clip_now, slot_now, pair_now = attention_unit(step, places, clips, pairs)
+
+    def attend_single():
+        clip, slot, pair = 0, slot_now, pair_now
 
         @pl.when((pair == 0) & (slot == 0))
         def own_grads():
@@ -738,29 +754,16 @@
         def vert_grads():
             grad_vert(clip).wait_recv()
 
-        query = q_ref[0]
-        keys = k_ref[0]
-        values = v_ref[0]
+        at = pl.ds(pl.multiple_of(slot * rows, rows), rows)
+        query, keys, values, live = q_ref[0, at], k_ref[0], v_ref[0], mask_ref[0] > 0.5
         grad = grad_all[slot, clip, :, lane_slice(pair * lanes, lanes)]
-        live = mask_ref[0] > 0.5
-        product = grad.astype(f32) * part_ref[0].astype(f32)
-        dqs, dk, dv = [], None, None
+        dqs, dk, dv = [], 0.0, 0.0
         for head in range(2):
-            own_query = only(query, head)
-            own_grad = only(grad, head)
-            scores = jnp.where(live, dot(own_query, keys, NT), MASKED)
-            probs = jnp.exp(scores - lse_ref[0, :, head * DH : head * DH + 1])
-            delta = jnp.sum(only(product, head), axis=1, keepdims=True)
-            dscores = (probs * (dot(own_grad, values, NT) - delta)).astype(bf16)
-            dqs.append(dot(dscores, keys))
-            more_k = dot(dscores, own_query, TN)
-            more_v = dot(probs.astype(bf16), own_grad, TN)
-            dk = more_k if dk is None else dk + more_k
-            dv = more_v if dv is None else dv + more_v
-        first = own_lanes(dqs[0].shape, 0)
-        dq = (jnp.where(first, dqs[0], dqs[1]) * DH ** -0.5).astype(bf16)
-        at = pl.ds(pl.multiple_of(slot * rows, rows), rows)
-        packed[clip, at, lane_slice(3 * pair * lanes, lanes)] = dq
+            probs, dscores, dq = head_back(head, query, keys, values, grad, part_ref[0, at], lse_ref[0, at], live)
+            dqs.append(dq)
+            dk = dk + dot(dscores, only(query, head), TN)
+            dv = dv + dot(probs, only(grad, head), TN)
+        packed[clip, at, lane_slice(3 * pair * lanes, lanes)] = join_heads(dqs)
 
         @pl.when(slot == 0)
         def keep():
@@ -769,20 +772,43 @@
 
         @pl.when(slot == 1)
         def send():
-            @pl.when(clip > 0)
-            def free():
-                kv_copy(clip - 1, pair).wait_send()
-
-            for part, value in enumerate((dk, dv)):
-                low = (kv_acc[pair, part] + value).astype(bf16)
-                packed[clip, :, lane_slice((3 * pair + part + 1) * lanes, lanes)] = low[: 2 * rows]
-                kv_send[pair, part] = low[2 * rows :]
-            kv_copy(clip, pair).start()
+            send_pair(clip, pair, kv_acc[pair, 0] + dk, kv_acc[pair, 1] + dv)
+
+    def attend_double():
+        clip, pair = clip_now, pair_now
+
+        @pl.when(pair == 0)
+        def grads():
+            grad_own(clip).wait()
+            grad_vert(clip).wait_recv()
+
+        kv_copy(clip - 1, pair).wait_send()
+        keys, values, live = k_ref[0], v_ref[0], mask_ref[0] > 0.5
+        here = lane_slice(pair * lanes, lanes)
+        query = q_ref[0]
+        grad = jnp.concatenate([grad_all[0, clip, :, here], grad_all[1, clip, :, here]], axis=0)
+        dqs, dk, dv = [[], []], 0.0, 0.0
+        for head in range(2):
+            parts = []
+            for slot in range(2):
+                at = slice(slot * rows, (slot + 1) * rows)
+                parts.append(
+                    head_back(head, query[at], keys, values, grad[at], part_ref[0, at], lse_ref[0, at], live)
+                )
+                dqs[slot].append(parts[slot][2])
+            probs, dscores = [jnp.concatenate([parts[0][i], parts[1][i]], axis=0) for i in range(2)]
+            dk = dk + dot(dscores, only(query, head), TN)
+            dv = dv + dot(probs, only(grad, head), TN)
+        for slot in range(2):
+            at = slice(slot * rows, (slot + 1) * rows)
+            packed[clip, at, lane_slice(3 * pair * lanes, lanes)] = join_heads(dqs[slot])
+        send_pair(clip, pair, dk, dv)
 
     is_attention = step < places["projections"][-1]
     for at in places["pauses"]:
         is_attention = is_attention & (step != at)
-    pl.when(is_attention)(attend)
+    pl.when(step < 2 * pairs)(attend_single)
+    pl.when(is_attention & (step >= 2 * pairs))(attend_double)
 
     def take_pair(clip, pair):
         kv_copy(clip, pair).wait_recv()
@@ -911,12 +937,17 @@
 
 
 def step_places(clips, pairs):
-    of_clip = 2 * pairs
-    projections = [of_clip * (c + 1) + 2 + c for c in range(clips - 1)]
-    begin = of_clip * (clips - 1) + clips - 1
-    chunks = [begin + 2 * (pair + 1) + 1 + pair for pair in range(pairs - 1)]
-    projections.append(begin + of_clip + pairs - 1)
-    inputs = projections[-1] + 1
+    plan = ["attend"] * (2 * pairs)
+    for clip in range(1, clips):
+        for pair in range(pairs):
+            plan.append("attend")
+            if pair == 0:
+                plan.append("project")
+            elif clip == clips - 1:
+                plan.append("chunk")
+    projections = [i for i, kind in enumerate(plan) if kind == "project"] + [len(plan)]
+    chunks = [i for i, kind in enumerate(plan) if kind == "chunk"]
+    inputs = len(plan) + 1
     pauses = projections[:-1] + chunks
     return {"projections": projections, "chunks": chunks, "pauses": pauses, "inputs": inputs, "end": inputs + clips - 1}
 
@@ -925,11 +956,10 @@
     index = step
     for at in places["pauses"]:
         index = index - (step > at).astype(jnp.int32)
-    index = jnp.minimum(index, 2 * clips * pairs - 1)
-    clip = index // (2 * pairs)
-    inside = index % (2 * pairs)
-    last = clip == clips - 1
-    return clip, jnp.where(last, inside % 2, inside // pairs), jnp.where(last, inside // 2, inside % pairs)
+    index = jnp.minimum(index, (clips + 1) * pairs - 1)
+    slot = jnp.where(index < 2 * pairs, index // pairs, 0)
+    clip = jnp.maximum(index // pairs - 1, 0)
+    return clip, slot, index % pairs
 
 
 def backward(q, k, v, mask, part, lse, normed, weight_half, tokens, far, gmid, gain, small, db1, gmixed,
@@ -947,10 +977,7 @@
     one = pl.Buffered(buffer_count=1)
 
     def of_pair(s):
-        return attention_unit(s, places, clips, pairs)
-
-    def of_keys(s):
-        clip, _, pair = of_pair(s)
+        clip, _, pair = attention_unit(s, places, clips, pairs)
         return clip, 0, pair
 
     def of_projection(s):
@@ -963,8 +990,8 @@
         return jnp.clip(s - places["inputs"], 0, clips - 1), 0, 0
 
     fixed = lambda shape: pl.BlockSpec(shape, lambda s: (0,) * len(shape), pipeline_mode=one)
-    tok_pair = pl.BlockSpec((1, rows, lanes), of_pair)
-    key_pair = pl.BlockSpec((1, keys, lanes), of_keys)
+    tok_pair = pl.BlockSpec((1, 2 * rows, lanes), of_pair)
+    key_pair = pl.BlockSpec((1, keys, lanes), of_pair)
     anywhere = pl.BlockSpec(memory_space=pl.ANY)
     blocks = (2,) * bits
     r_fc1, r_fc2 = width // clip_size, hidden // clip_size
@@ -1011,8 +1038,8 @@
             tok_pair, tok_pair,
             pl.BlockSpec((1, 2 * rows, width), of_projection),
             fixed(weight_half.shape),
-            pl.BlockSpec((1, slots, width), of_projection),
-            pl.BlockSpec((1, rows, width), of_projection),
+            pl.BlockSpec((1, slots, width), of_projection, pipeline_mode=one),
+            pl.BlockSpec((1, rows, width), of_projection, pipeline_mode=one),
             pl.BlockSpec((1, slots, width), of_clip),
             pl.BlockSpec((1, rows, width), of_clip),
             fixed((width,)), fixed((8, width)), fixed((1, hidden)),
@@ -1032,7 +1059,9 @@
             shape((16, width), f32),
         ],
         scratch_shapes=scratch,
-        compiler_params=params(collective_id=1, has_side_effects=True),
+        compiler_params=pltpu.CompilerParams(
+            vmem_limit_bytes=63 * 1024 * 1024, collective_id=1, has_side_effects=True
+        ),
         cost_estimate=pl.CostEstimate(
             flops=2 * clips * rows * (5 * keys * width + 6 * width * width),
             bytes_accessed=60_000_000,

time: 222 us -> 213 us (0.959)
  Pallas kernels: 221 us -> 212 us
    pallas_call x1, Pallas kernels: 114 us -> 105 us  [backward(): pl.pallas_call(functools.partial(backward_kernel, (clips, slots, rows, bi...]
where the time goes in v5:
time: 213 us
  Pallas kernels  212 us (100%)
    pallas_call x1, Pallas kernels, backward(): pl.pallas_call(functools.partial(backward_kernel, (clips, slots, rows, bi...  105 us
    pallas_call x1, Pallas kernels, forward(): pl.pallas_call(functools.partial(forward_kernel, (clips, slots, rows, pai...  61.2 us
    pallas_call x1, Pallas kernels, mlp(): pl.pallas_call(functools.partial(mlp_kernel, (clips, slots, rows, tile)),...  39.8 us
    pallas_call x1, Pallas kernels, final_outputs(): pl.pallas_call(outputs_kernel, grid=(steps,), in_specs=[by_rows(a) for a...  5.84 us

profile of v5, /device:TPU:0, one launch (start us, length us, event | category | flops | bytes accessed | tf_op | source)
XLA Modules:
  0.0 212.8 jit_solution(7615248231752136502)
XLA Ops:
  0.6 61.2 %forward.1 = (bf16[3,608,384]{2,1,0:T(8,128)(2,1)}, bf16[3,1216,384]{2,1,0:T(8,128)(2,1)}, bf16[3,1216,384]{2,1,0:T(8,128)(2,1)}, bf16[3,608,768]{2,1,0:T(8,128)...) custom-call(s32[3]{0:T(128)} %bitcast.9, ...), custom_call_target="tpu_custom_call" | custom-call | flops 9861857280 | bytes 40000000 | tf_op jit(solution)/shard_map/forward/pallas_call | solution.py:288
  61.8 39.8 %mlp.1 = (bf16[3,298,768]{2,1,0:T(8,128)(2,1)}, bf16[2,768,1536]{2,1,0:T(8,128)(2,1)}, bf16[2,3072,384]{2,1,0:T(8,128)(2,1)}, bf16[2,768,384]{2,1,0:T(8,128)(2,1...) custom-call(s32[3]{0:T(128)} %bitcast.10, ...), custom_call_target="tpu_custom_call" | custom-call | flops 25820135424 | bytes 40000000 | tf_op jit(solution)/shard_map/mlp/pallas_call | solution.py:460
  101.7 105.1 %backward.1 = (f32[3,298,768]{2,1,0:T(8,128)}, bf16[96,3072]{1,0:T(8,128)(2,1)}, bf16[384,768]{1,0:T(8,128)(2,1)}, bf16[96,768]{1,0:T(8,128)(2,1)}, bf16[96,2304]{1,0:T(8,128)(2,1)}, /*index=5*/f32[16,768]{1,0:T(8,128)}) custom-call(bf16[3,608,384]{2,1,0:T(8,128)(2,1)} %get-tuple-element.59.q_ref, bf16[3,1216,384]{2,1,0:T(8,128)(2,1)} %get-tuple-element.60.k_ref, ...), custom_call_target="tpu_custom_call" | custom-call | flops 14972092416 | bytes 60000000 | tf_op jit(solution)/shard_map/backward/pallas_call | solution.py:1032
  206.8 5.8 %final_outputs.1 = (f32[96,3072]{1,0:T(8,128)}, f32[384,768]{1,0:T(8,128)}, f32[96,768]{1,0:T(8,128)}, f32[96,2304]{1,0:T(8,128)}, f32[3,298,768]{2,1,0:T(8,128)...) custom-call(bf16[96,3072]{1,0:T(8,128)(2,1)} %get-tuple-element.75.f, ...), custom_call_target="tpu_custom_call" | custom-call | tf_op jit(solution)/shard_map/final_outputs/pallas_call | solution.py:1102

commit v6 on v5

--- a/solution.py
+++ b/solution.py
@@ -527,33 +527,35 @@
     ] + chunks
 
 
-PROJ_ORDER = (0, 1, 2)
+PROJ_ORDER = (1, 0, 2)
 QKV_ORDERS = ((0, 1, 2), (0, 1, 2), (1, 0, 2))
 SUM_STEPS = {
-    2: [("end", 0, 0), ("start", 0, 1), ("end", 1, 0), ("start", 1, 1)],
-    3: [("end", 2, 0)],
-    4: [("end", 3, 0), ("end", 4, 0)],
-    6: [("start", 2, 1), ("start", 3, 1)],
-    7: [("end", 0, 1), ("end", 1, 1)],
-    9: [("end", 2, 1), ("start", 0, 2), ("start", 1, 2), ("end", 3, 1)],
-    10: [("start", 2, 2), ("start", 3, 2)],
-    11: [("end", 0, 2), ("start", 0, 3), ("end", 1, 2)],
-    12: [("end", 2, 2), ("start", 1, 3), ("start", 4, 1), ("end", 3, 2)],
-    13: [("end", 0, 3), ("start", 0, 4), ("start", 2, 3)],
-    15: [("end", 5, 0), ("start", 5, 1), ("start", 3, 3), ("end", 0, 4), ("start", 0, 5),
-        ("end", 1, 3), ("start", 1, 4), ("end", 4, 1)],
-    16: [("end", 0, 5), ("start", 4, 2), ("end", 2, 3), ("start", 2, 4)],
-    17: [("end", 5, 1), ("start", 5, 2), ("end", 6, 0), ("start", 6, 1), ("end", 7, 0),
-        ("start", 7, 1), ("end", 1, 4), ("start", 1, 5), ("end", 2, 4), ("start", 2, 5),
-        ("end", 3, 3), ("start", 3, 4), ("end", 4, 2), ("start", 4, 3)],
-    18: [("end", 1, 5), ("end", 2, 5)],
-    19: [("end", 5, 2), ("start", 5, 3), ("vec", 0, 0), ("end", 6, 1), ("start", 6, 2), ("end", 7, 1),
-        ("start", 7, 2), ("end", 4, 3), ("start", 4, 4), ("vec", 1, 0), ("input", 2, 0),
-        ("end", 6, 2), ("start", 6, 3), ("end", 5, 3), ("start", 5, 4), ("end", 7, 2),
-        ("start", 7, 3), ("end", 3, 4), ("start", 3, 5), ("vec", 2, 0), ("end", 4, 4),
-        ("start", 4, 5), ("end", 3, 5), ("end", 5, 4), ("start", 5, 5), ("end", 4, 5), ("end", 6, 3),
-        ("start", 6, 4), ("end", 5, 5), ("end", 7, 3), ("start", 7, 4), ("vec", 3, 0), ("end", 6, 4),
-        ("start", 6, 5), ("end", 7, 4), ("start", 7, 5), ("end", 6, 5), ("end", 7, 5), ("vec", 4, 0)],
+    2: [("end", 0, 0), ("start", 0, 1)],
+    3: [("end", 1, 0), ("start", 1, 1)],
+    4: [("end", 2, 0), ("end", 3, 0), ("end", 4, 0)],
+    6: [("start", 2, 1)],
+    7: [("end", 0, 1), ("start", 0, 2)],
+    8: [("end", 1, 1), ("start", 3, 1)],
+    9: [("start", 1, 2)],
+    10: [("end", 0, 2), ("start", 0, 3), ("end", 2, 1)],
+    11: [("start", 2, 2)],
+    12: [("end", 1, 2), ("start", 1, 3), ("end", 3, 1), ("start", 3, 2)],
+    13: [("end", 0, 3), ("start", 0, 4), ("start", 4, 1)],
+    14: [("end", 2, 2), ("start", 2, 3)],
+    15: [("end", 5, 0), ("start", 5, 1), ("end", 1, 3), ("start", 1, 4), ("end", 3, 2)],
+    16: [("end", 0, 4), ("start", 0, 5), ("start", 3, 3)],
+    17: [("end", 5, 1), ("start", 5, 2), ("end", 6, 0), ("start", 6, 1), ("end", 0, 5), ("end", 1, 4),
+        ("start", 1, 5), ("end", 2, 3), ("start", 2, 4), ("end", 4, 1)],
+    18: [("end", 7, 0), ("start", 7, 1), ("start", 4, 2)],
+    19: [("end", 1, 5), ("vec", 0, 0), ("end", 3, 3), ("start", 3, 4), ("end", 5, 2), ("start", 5, 3),
+        ("end", 6, 1), ("start", 6, 2), ("end", 7, 1), ("start", 7, 2), ("end", 4, 2),
+        ("start", 4, 3), ("vec", 1, 0), ("input", 2, 0), ("end", 5, 3), ("start", 5, 4),
+        ("end", 2, 4), ("start", 2, 5), ("end", 6, 2), ("start", 6, 3), ("end", 7, 2),
+        ("start", 7, 3), ("end", 3, 4), ("start", 3, 5), ("end", 2, 5), ("vec", 2, 0), ("end", 4, 3),
+        ("start", 4, 4), ("end", 5, 4), ("start", 5, 5), ("end", 3, 5), ("end", 6, 3),
+        ("start", 6, 4), ("end", 5, 5), ("end", 7, 3), ("start", 7, 4), ("end", 4, 4),
+        ("start", 4, 5), ("vec", 3, 0), ("end", 6, 4), ("start", 6, 5), ("end", 4, 5), ("end", 7, 4),
+        ("start", 7, 5), ("end", 6, 5), ("vec", 4, 0), ("end", 7, 5)],
 }
 
 

time: 213 us -> 212 us (level)
  no operation moved by 1% of the time
where the time goes in v6:
time: 212 us
  Pallas kernels  211 us (100%)
    pallas_call x1, Pallas kernels, backward(): pl.pallas_call(functools.partial(backward_kernel, (clips, slots, rows, bi...  104 us
    pallas_call x1, Pallas kernels, forward(): pl.pallas_call(functools.partial(forward_kernel, (clips, slots, rows, pai...  61.2 us
    pallas_call x1, Pallas kernels, mlp(): pl.pallas_call(functools.partial(mlp_kernel, (clips, slots, rows, tile)),...  39.8 us
    pallas_call x1, Pallas kernels, final_outputs(): pl.pallas_call(outputs_kernel, grid=(steps,), in_specs=[by_rows(a) for a...  5.84 us

profile of v6, /device:TPU:0, one launch (start us, length us, event | category | flops | bytes accessed | tf_op | source)
XLA Modules:
  0.0 212.0 jit_solution(10296533415871703997)
XLA Ops:
  0.6 61.2 %forward.1 = (bf16[3,608,384]{2,1,0:T(8,128)(2,1)}, bf16[3,1216,384]{2,1,0:T(8,128)(2,1)}, bf16[3,1216,384]{2,1,0:T(8,128)(2,1)}, bf16[3,608,768]{2,1,0:T(8,128)...) custom-call(s32[3]{0:T(128)} %bitcast.9, ...), custom_call_target="tpu_custom_call" | custom-call | flops 9861857280 | bytes 40000000 | tf_op jit(solution)/shard_map/forward/pallas_call | solution.py:288
  61.8 39.8 %mlp.1 = (bf16[3,298,768]{2,1,0:T(8,128)(2,1)}, bf16[2,768,1536]{2,1,0:T(8,128)(2,1)}, bf16[2,3072,384]{2,1,0:T(8,128)(2,1)}, bf16[2,768,384]{2,1,0:T(8,128)(2,1...) custom-call(s32[3]{0:T(128)} %bitcast.10, ...), custom_call_target="tpu_custom_call" | custom-call | flops 25820135424 | bytes 40000000 | tf_op jit(solution)/shard_map/mlp/pallas_call | solution.py:460
  101.7 104.3 %backward.1 = (f32[3,298,768]{2,1,0:T(8,128)}, bf16[96,3072]{1,0:T(8,128)(2,1)}, bf16[384,768]{1,0:T(8,128)(2,1)}, bf16[96,768]{1,0:T(8,128)(2,1)}, bf16[96,2304]{1,0:T(8,128)(2,1)}, /*index=5*/f32[16,768]{1,0:T(8,128)}) custom-call(bf16[3,608,384]{2,1,0:T(8,128)(2,1)} %get-tuple-element.59.q_ref, bf16[3,1216,384]{2,1,0:T(8,128)(2,1)} %get-tuple-element.60.k_ref, ...), custom_call_target="tpu_custom_call" | custom-call | flops 14972092416 | bytes 60000000 | tf_op jit(solution)/shard_map/backward/pallas_call | solution.py:1034
  206.0 5.8 %final_outputs.1 = (f32[96,3072]{1,0:T(8,128)}, f32[384,768]{1,0:T(8,128)}, f32[96,768]{1,0:T(8,128)}, f32[96,2304]{1,0:T(8,128)}, f32[3,298,768]{2,1,0:T(8,128)...) custom-call(bf16[96,3072]{1,0:T(8,128)(2,1)} %get-tuple-element.75.f, ...), custom_call_target="tpu_custom_call" | custom-call | tf_op jit(solution)/shard_map/final_outputs/pallas_call | solution.py:1104

commit v7 on v6

--- a/solution.py
+++ b/solution.py
@@ -703,6 +703,12 @@
             grad_own(clip).start()
         for device in [core_dev, vert_dev] + clip_dev:
             pl.semaphore_signal(barrier, inc=1, device_id=device, device_id_type=mesh_id)
+        vec_sum[0] = jnp.zeros_like(vec_sum[0])
+        bias_acc[...] = jnp.zeros_like(bias_acc)
+        dw_acc[...] = jnp.zeros_like(dw_acc)
+        vec_sum[0, 4:8] = small_ref[0:4]
+        for i in range(db1_ref.shape[1] // width):
+            vec_sum[0, 8 + i : 9 + i] = db1_ref[0:1, i * width : (i + 1) * width]
         pl.semaphore_wait(barrier, 2 + bits)
         for clip in range(clips):
             grad_vert(clip).start()
@@ -710,12 +716,6 @@
             stage_copy(a, 0).start()
         for a in (0, 1, 4):
             own_copy(a).start()
-        vec_sum[0] = jnp.zeros_like(vec_sum[0])
-        bias_acc[...] = jnp.zeros_like(bias_acc)
-        dw_acc[...] = jnp.zeros_like(dw_acc)
-        vec_sum[0, 4:8] = small_ref[0:4]
-        for i in range(db1_ref.shape[1] // width):
-            vec_sum[0, 8 + i : 9 + i] = db1_ref[0:1, i * width : (i + 1) * width]
 
     for at in sorted(SUM_STEPS):
         if at < places["end"]:

time: 212 us -> 212 us (level)
  no operation moved by 1% of the time
where the time goes in v7:
time: 212 us
  Pallas kernels  211 us (100%)
    pallas_call x1, Pallas kernels, backward(): pl.pallas_call(functools.partial(backward_kernel, (clips, slots, rows, bi...  104 us
    pallas_call x1, Pallas kernels, forward(): pl.pallas_call(functools.partial(forward_kernel, (clips, slots, rows, pai...  61.2 us
    pallas_call x1, Pallas kernels, mlp(): pl.pallas_call(functools.partial(mlp_kernel, (clips, slots, rows, tile)),...  39.8 us
    pallas_call x1, Pallas kernels, final_outputs(): pl.pallas_call(outputs_kernel, grid=(steps,), in_specs=[by_rows(a) for a...  5.84 us

profile of v7, /device:TPU:0, one launch (start us, length us, event | category | flops | bytes accessed | tf_op | source)
XLA Modules:
  0.0 211.6 jit_solution(4876682068406540510)
XLA Ops:
  0.6 61.2 %forward.1 = (bf16[3,608,384]{2,1,0:T(8,128)(2,1)}, bf16[3,1216,384]{2,1,0:T(8,128)(2,1)}, bf16[3,1216,384]{2,1,0:T(8,128)(2,1)}, bf16[3,608,768]{2,1,0:T(8,128)...) custom-call(s32[3]{0:T(128)} %bitcast.9, ...), custom_call_target="tpu_custom_call" | custom-call | flops 9861857280 | bytes 40000000 | tf_op jit(solution)/shard_map/forward/pallas_call | solution.py:288
  61.8 39.8 %mlp.1 = (bf16[3,298,768]{2,1,0:T(8,128)(2,1)}, bf16[2,768,1536]{2,1,0:T(8,128)(2,1)}, bf16[2,3072,384]{2,1,0:T(8,128)(2,1)}, bf16[2,768,384]{2,1,0:T(8,128)(2,1...) custom-call(s32[3]{0:T(128)} %bitcast.10, ...), custom_call_target="tpu_custom_call" | custom-call | flops 25820135424 | bytes 40000000 | tf_op jit(solution)/shard_map/mlp/pallas_call | solution.py:460
  101.7 103.9 %backward.1 = (f32[3,298,768]{2,1,0:T(8,128)}, bf16[96,3072]{1,0:T(8,128)(2,1)}, bf16[384,768]{1,0:T(8,128)(2,1)}, bf16[96,768]{1,0:T(8,128)(2,1)}, bf16[96,2304]{1,0:T(8,128)(2,1)}, /*index=5*/f32[16,768]{1,0:T(8,128)}) custom-call(bf16[3,608,384]{2,1,0:T(8,128)(2,1)} %get-tuple-element.59.q_ref, bf16[3,1216,384]{2,1,0:T(8,128)(2,1)} %get-tuple-element.60.k_ref, ...), custom_call_target="tpu_custom_call" | custom-call | flops 14972092416 | bytes 60000000 | tf_op jit(solution)/shard_map/backward/pallas_call | solution.py:1034
  205.6 5.8 %final_outputs.1 = (f32[96,3072]{1,0:T(8,128)}, f32[384,768]{1,0:T(8,128)}, f32[96,768]{1,0:T(8,128)}, f32[96,2304]{1,0:T(8,128)}, f32[3,298,768]{2,1,0:T(8,128)...) custom-call(bf16[96,3072]{1,0:T(8,128)(2,1)} %get-tuple-element.75.f, ...), custom_call_target="tpu_custom_call" | custom-call | tf_op jit(solution)/shard_map/final_outputs/pallas_call | solution.py:1104
